TPU v7x, 32 devices: a whole 2x2x4 slice. The times are simulated.
32 devices in a mesh: section: 4 (over z), dp: 2 (over x), tensor: 4 (over y, core).
Axes of the slice: x: 2, y: 2, z: 4, core: 2. Of those that a mesh axis runs over, the one named last changes fastest.
Arguments:
- hidden: bfloat16 [64, 16384], P(('section', 'dp'), 'tensor'), may hold values from -100 to 100
- norm_gain: float32 [16384], replicated, may hold values from 0.5 to 1.5
- head_weight: bfloat16 [8192, 16384], P(('section', 'dp', 'tensor')), may hold values from -100 to 100
- token_ids: int32 [64], P(('section', 'dp')), may hold values from 0 to 8191
- resp_len: int32 [8, 2], P(('section', 'dp')), may hold values from 1 to 4, 6 in all within a row
- group_of: int32 [8, 2], P(('section', 'dp')), may hold values from 0 to 7
- loss_mask: int32 [64], P(('section', 'dp', 'tensor')), may hold values 0 or 1
- old_logp: float32 [64], P(('section', 'dp', 'tensor')), may hold values from -30 to 0
- ref_logp: float32 [64], P(('section', 'dp', 'tensor')), may hold values from -30 to 0
- advantage: float32 [64], P(('section', 'dp', 'tensor')), may hold values from -30 to 30
Outputs:
- token_logp: float32 [64], P(('section', 'dp', 'tensor'))
- group_loss: float32 [8], replicated
- group_count: float32 [8], replicated
Inputs may be any that keep to these rules, and one draw needn't show every extreme that they name: `resp_len`: the response lengths of the 2 sequences of each shard sum to exactly 6.
All inputs are finite; a program needn't handle non-finite values. No bound on the sum of `loss_mask` on one device may be relied on, other than what follows from the above.
Results may differ from a plain program's by a relative error of at most 0.0003.
The roundings to bfloat16 on the way count: a program that leaves them out, or rounds other values in their place, can miss the bound.
Values may be sent and summed in bfloat16 or wider, within the bound.
No kernel may reach another device: no remote copies, remote signals or barrier semaphores. Data moves between devices by JAX's collectives and lax.ppermute only.
A program may use at most 128 MiB of HBM per device.

v0:
```python
import jax
import jax.numpy as jnp
from jax import lax
from jax.sharding import PartitionSpec as P

D = 16384
GROUPS = 8


epsilon = 1e-05
clip_range = 0.2
kl_weight = 0.1
log_clamp = 20.0


def combined_all(part, axis, combine):
    gathered = jax.tree.map(lambda a: lax.all_gather(a, axis), part)

    def take(source):
        return jax.tree.map(lambda a: lax.dynamic_index_in_dim(a, source, 0, False), gathered)

    return lax.fori_loop(
        1, lax.axis_size(axis), lambda source, state: combine(state, take(source)), take(0)
    )


def token_loss(logprob, old_logp, ref_logp, advantage, weight):
    ratios = jnp.exp(logprob - old_logp)
    clipped = jnp.clip(ratios, 1.0 - clip_range, 1.0 + clip_range)
    surrogate = jnp.minimum(ratios * advantage, clipped * advantage)
    log_gap = jnp.clip(ref_logp - logprob, -log_clamp, log_clamp)
    penalty = jnp.exp(log_gap) - log_gap - 1.0
    return (kl_weight * penalty - surrogate) * weight


def layout(lengths, row_count):
    local_row = jnp.arange(row_count, dtype=jnp.int32)
    seq_count = lengths.shape[0]
    window = row_count // seq_count
    seq_num = local_row // window
    within = local_row % window
    member = seq_num[:, None] == jnp.arange(seq_count, dtype=jnp.int32)[None, :]
    length_row = jnp.sum(jnp.where(member, lengths[None, :], 0), axis=1)
    before = jnp.cumsum(lengths) - lengths
    offset = jnp.sum(jnp.where(member, before[None, :], 0), axis=1)
    is_live = within >= window - length_row
    live_rank = offset + within - (window - length_row)
    return (member, is_live, live_rank)


def local(
    hidden,
    norm_gain,
    head_weight,
    token_ids,
    resp_len,
    group_of,
    loss_mask,
    old_logp,
    ref_logp,
    advantage,
):
    row_count = hidden.shape[0]
    member, is_live, live_rank = layout(resp_len[0], row_count)
    width_part = hidden.shape[1]
    tensor_idx = lax.axis_index("tensor")
    gain_part = lax.dynamic_slice_in_dim(norm_gain, tensor_idx * width_part, width_part)
    values = hidden.astype(jnp.float32)
    square_sum = lax.psum(jnp.sum(values * values, axis=1), "tensor")
    mean_square = square_sum / D
    outgoing = (values * lax.rsqrt(mean_square + epsilon)[:, None] * gain_part[None, :]).astype(
        jnp.bfloat16
    )
    gathered = lax.all_gather(outgoing, "tensor", axis=1, tiled=True)
    vocab_rows = head_weight.shape[0]
    columns = lax.axis_index(("section", "dp", "tensor")) * vocab_rows + jnp.arange(
        vocab_rows, dtype=jnp.int32
    )
    piece_rows = lax.all_gather(gathered, ("section", "dp"), axis=0, tiled=True)
    piece_ids = lax.all_gather(token_ids, ("section", "dp"), axis=0, tiled=True)
    logits = jnp.einsum("rd,vd->rv", piece_rows, head_weight, preferred_element_type=jnp.float32)
    row_max = jnp.max(logits, axis=1)
    totals = jnp.sum(jnp.exp(logits - row_max[:, None]), axis=1)
    chosen = jnp.sum(jnp.where(piece_ids[:, None] == columns[None, :], logits, 0.0), axis=1)
    stats = (row_max, totals, chosen)

    def combine(earlier, later):
        new_max = jnp.maximum(earlier[0], later[0])
        totals = earlier[1] * jnp.exp(earlier[0] - new_max) + later[1] * jnp.exp(later[0] - new_max)
        return (new_max, totals, earlier[2] + later[2])

    row_max, totals, chosen = combined_all(stats, ("section", "dp", "tensor"), combine)
    log_total = row_max + jnp.log(totals)
    own_count = loss_mask.shape[0]
    own_start = tensor_idx * own_count
    own_live = lax.dynamic_slice_in_dim(is_live, own_start, own_count)
    own_member = lax.dynamic_slice_in_dim(member, own_start, own_count, 0)
    shard_idx = lax.axis_index(("section", "dp"))
    lookup = shard_idx * row_count + own_start + jnp.arange(own_count, dtype=jnp.int32)
    logprob = chosen[lookup] - log_total[lookup]
    token_logp = jnp.where(own_live, logprob, 0.0)
    weight = own_live.astype(jnp.float32) * loss_mask.astype(jnp.float32)
    losses = token_loss(logprob, old_logp, ref_logp, advantage, weight)
    own_group = jnp.sum(jnp.where(own_member, group_of[0][None, :], 0), axis=1)
    group_hit = (own_group[:, None] == jnp.arange(GROUPS, dtype=jnp.int32)[None, :]).astype(
        jnp.float32
    )
    group_loss, group_count = lax.psum(
        (
            jnp.sum(group_hit * losses[:, None], axis=0),
            jnp.sum(group_hit * weight[:, None], axis=0),
        ),
        ("section", "dp", "tensor"),
    )
    return (token_logp, group_loss, group_count)


def solution(mesh):
    return jax.shard_map(
        local,
        mesh=mesh,
        in_specs=(
            P(("section", "dp"), "tensor"),
            P(),
            P(("section", "dp", "tensor"), None),
            P(("section", "dp")),
            P(("section", "dp"), None),
            P(("section", "dp"), None),
            P(("section", "dp", "tensor")),
            P(("section", "dp", "tensor")),
            P(("section", "dp", "tensor")),
            P(("section", "dp", "tensor")),
        ),
        out_specs=(P(("section", "dp", "tensor")), P(), P()),
        check_vma=False,
    )
```

profile of v0, /device:TPU:0, one launch (start us, length us, event | category | flops | bytes accessed | tf_op | source)
XLA Modules:
  0.0 171.9 jit_solution(11519364338927570524)
XLA Ops:
  7.2 0.0 copy-start.3
  7.2 0.0 copy-start.1
  7.2 0.0 copy-start.2
  7.2 0.0 copy-start
  7.2 0.0 all-gather.5.cloned.1.call-start
  7.3 1.0 fusion.7
  8.2 8.4 %psum.21 = f32[8]{0:T(128)S(1)} all-reduce(f32[8]{0:T(128)S(1)} %fusion.7), channel_id=1, replica_groups=mesh['section'=4,'dp'=2,'tensor'=4] {'tensor'}, use_global_device_ids=true, to_apply=%region_2.3 | all-reduce | flops 8 | bytes 64 | tf_op jit(solution)/shard_map/psum | solution.py:69
  16.6 0.7 dynamic_slice.50
  17.4 0.9 fusion.9
  18.3 6.2 %all_gather.27 = bf16[8,16384]{1,0:T(8,128)(2,1)} all-gather(bf16[8,4096]{1,0:T(8,128)(2,1)S(1)} %fusion.9), channel_id=1, replica_groups=mesh['section'=4,'dp'=2,'tensor'=4] {'tensor'}, dimensions={1}, use_global_device_ids=true | all-gather | bytes 327680 | tf_op jit(solution)/shard_map/all_gather | solution.py:74
  24.5 0.0 all-gather.5.cloned.1.call-update
  24.6 1.2 dynamic-slice
  26.5 0.9 dynamic-update-slice.2
  27.3 11.8 %all-reduce.2 = s32[64]{0:T(128)S(1)} all-reduce(s32[64]{0:T(128)S(1)} %dynamic-update-slice.2), channel_id=1, replica_groups=mesh['section'=4,'dp'=2,'tensor'=4] {'section','dp'}, use_global_device_ids=true, to_apply=%add.2 | all-reduce | flops 64 | bytes 512
  39.2 0.1 iota_compare_fusion
  39.3 0.8 fusion.10
  40.0 0.8 select_reduce_fusion.1
  40.9 33.2 %all-gather.5.cloned.1.call-done = bf16[64,16384]{1,0:T(8,128)(2,1)} async-done(((bf16[8,16384]{1,0:T(8,128)(2,1)}), bf16[64,16384]{1,0:T(8,128)(2,1)}) %all-gather.5.cloned.1.call-update) | async-done | bytes 2097168 | tf_op jit(solution)/shard_map/all_gather | solution.py:79
  74.1 6.8 %fusion.18 = (f32[64]{0:T(128)S(1)}, f32[64,256]{1,0:T(8,128)S(1)}) fusion(bf16[64,16384]{1,0:T(8,128)(2,1)} %all-gather.5.cloned.1.call-done, bf16[256,16384]{1,0:T(8,128)(2,1)} %param.14), kind=kOutput, calls=%fused_computation.45 | convolution fusion | flops 536887232 | bytes 10551552 | tf_op jit(solution)/shard_map/rd,vd->rv/dot_general | solution.py:81
  80.9 0.3 dynamic-update-slice
  81.2 0.2 select_reduce_fusion
  81.4 0.3 dynamic-update-slice.3
  81.7 0.3 dynamic-update-slice.1
  82.0 39.5 %all-reduce.5 = (f32[2048]{0:T(1024)S(1)}, f32[2048]{0:T(1024)S(1)}, f32[2048]{0:T(1024)S(1)}) all-reduce(f32[2048]{0:T(1024)S(1)} %dynamic-update-slice, f32[2048]{0:T(1024)S(1)} %dynamic-update-slice.1, f32[2048]{0:T(1024)S(1)} %dynamic-update-slice.3), channel_id=2, replica_groups=mesh['section'=4,'dp'=2,'tensor'=4] {'section','dp','tensor'}, use_global_device_ids=true, to_apply=%add | all-reduce | flops 6144 | bytes 49152
  121.4 0.1 reshape.62
  121.5 0.1 reshape.63
  121.6 0.1 reshape.64
  121.7 1.4 while.19
  123.1 0.6 gather_fusion.1
  123.8 0.6 gather_fusion
  124.4 0.0 copy-done.3
  124.4 0.0 copy-done.1
  124.4 0.0 copy-done.2
  124.4 0.0 copy-done
  124.4 0.6 fusion.15
  125.0 0.1 select_reduce_fusion.2
  125.1 40.0 %all-reduce.4 = (f32[8]{0:T(128)}, f32[8]{0:T(128)}) all-reduce(f32[8]{0:T(128)S(1)} %get-tuple-element.187, f32[8]{0:T(128)S(1)} %get-tuple-element.186), channel_id=1, replica_groups=mesh['section'=4,'dp'=2,'tensor'=4] {'section','dp','tensor'}, use_global_device_ids=true, to_apply=%region_10.11 | all-reduce | flops 16 | bytes 128 | tf_op jit(solution)/shard_map/psum | solution.py:108
  (45 shorter events, 0.9 us)
Async XLA Ops:
  7.2 117.2 %copy-start.3 = (s32[2]{0:T(128)S(1)}, s32[2]{0:T(128)}, u32[]{:S(2)}) copy-start(s32[2]{0:T(128)} %param.18) | copy-start | bytes 28
  7.2 117.2 %copy-start.1 = (f32[2]{0:T(128)S(1)}, f32[2]{0:T(128)}, u32[]{:S(2)}) copy-start(f32[2]{0:T(128)} %param.19) | copy-start | bytes 28
  7.2 117.2 %copy-start.2 = (f32[2]{0:T(128)S(1)}, f32[2]{0:T(128)}, u32[]{:S(2)}) copy-start(f32[2]{0:T(128)} %param.20) | copy-start | bytes 28
  7.2 117.2 %copy-start = (f32[2]{0:T(128)S(1)}, f32[2]{0:T(128)}, u32[]{:S(2)}) copy-start(f32[2]{0:T(128)} %param.21) | copy-start | bytes 28
  7.2 66.9 %all-gather.5.cloned.1.call-start = ((), (), s32[]{:S(2)}) async-start(), calls=%async_computation | async-start | bytes 2359296 | tf_op jit(solution)/shard_map/all_gather | solution.py:79
Sparse Core Ops, SparseCore 0:
  24.7 49.4 all-gather.4
where the time goes:
time: 172 us
  blocking collectives  106 us (62%)
  waiting for transfers between devices  33.3 us (19%)
  between operations  14.8 us (9%)
  matrix products  6.78 us (4%)
  other arithmetic  5.37 us (3%)
  local copies, waits for them, and re-layouts  5.15 us (3%)
    unnamed x2, blocking collectives  51.3 us
    psum x1, blocking collectives, local(): lax.psum((jnp.sum(group_hit * losses[:, None], axis=0), jnp.sum(group_hit...  40 us
    all_gather x1, waiting for transfers between devices, local(): piece_rows = lax.all_gather(gathered, ('section', 'dp'), axis=0, tiled=True)  33.2 us
    psum x1, blocking collectives, local(): square_sum = lax.psum(jnp.sum(values * values, axis=1), 'tensor')  8.39 us
    dot_general x1, matrix products, local(): jnp.einsum('rd,vd->rv', piece_rows, head_weight, preferred_element_type=j...  6.78 us
    all_gather x1, blocking collectives, local(): gathered = lax.all_gather(outgoing, 'tensor', axis=1, tiled=True)  6.23 us
  transfers between devices with their start and end apart: 1, of which 1 were waited for; matrix products, arithmetic and copies ran while one was open for 2% of the time, Pallas kernels for 0%

commit v1 on v0

v1 whole, which is shorter than its diff:
```python
import jax
import jax.numpy as jnp
from jax import lax
from jax.experimental import pallas as pl
from jax.experimental.pallas import tpu as pltpu
from jax.sharding import PartitionSpec as P

GROUPS = 8
LANES = 128
FIELDS = 6
DIGITS = 3
BASE = 256

epsilon = 1e-05
clip_range = 0.2
kl_weight = 0.1
log_clamp = 20.0

ALL = ("section", "dp", "tensor")


def token_loss(logprob, old_logp, ref_logp, advantage, weight):
    ratios = jnp.exp(logprob - old_logp)
    clipped = jnp.clip(ratios, 1.0 - clip_range, 1.0 + clip_range)
    surrogate = jnp.minimum(ratios * advantage, clipped * advantage)
    log_gap = jnp.clip(ref_logp - logprob, -log_clamp, log_clamp)
    penalty = jnp.exp(log_gap) - log_gap - 1.0
    return (kl_weight * penalty - surrogate) * weight


def spread(x, axis, size, inner=1):
    if size == 1:
        return x
    length = lax.axis_size(axis)
    span = size * inner
    blocks = [x]
    for k in range(1, size):
        pairs = []
        for i in range(length):
            base, rest = i // span * span, i % span
            place, low = rest // inner, rest % inner
            pairs.append((i, base + (place + k) % size * inner + low))
        blocks.append(lax.ppermute(x, axis, pairs))
    return jnp.concatenate(blocks, axis=0)


def head_kernel(sizes, where, *refs):
    rows, half, sections, dps, ys, cores = sizes
    count = 2 * cores
    pieces = refs[:count]
    gain, extra, head, out, weights, normed, sems = refs[count:]
    section, dp, y, core, device = (where[i] for i in range(5))
    vocab = head.shape[0]
    tok = sections * dps * rows
    order = [(c, yr, h) for c in range(cores) for yr in range(ys) for h in range(2)]
    slots = []
    copies = []
    for n, (c, yr, h) in enumerate(order):
        slot = (lax.rem(y + ys - yr, ys) * cores + lax.rem(core + cores - c, cores)) * 2 + h
        slots.append(slot)
        copy = pltpu.make_async_copy(
            head.at[:, pl.ds(pl.multiple_of(slot * half, LANES), half)], weights.at[n], sems.at[n]
        )
        copy.start()
        copies.append(copy)

    def rows_of(n):
        c, yr, h = order[n]
        ref = pieces[c * 2 + h]
        if h == 0:
            size = dps * sections * rows
            return [(0, ref[yr * size : (yr + 1) * size, :half])]
        size = sections * rows
        return [
            (x * size, ref[(x * ys + yr) * size : (x * ys + yr + 1) * size, :half])
            for x in range(dps)
        ]

    def block(n):
        parts = [part for _, part in rows_of(n)]
        return parts[0] if len(parts) == 1 else jnp.concatenate(parts, axis=0)

    total = jnp.zeros((tok, LANES), jnp.float32)
    for n in range(len(order)):
        values = block(n).astype(jnp.float32)
        squares = values * values
        for start in range(0, half, LANES):
            total = total + squares[:, start : start + LANES]
    scale = lax.rsqrt(jnp.sum(total, axis=1, keepdims=True) / (len(order) * half) + epsilon)
    for n in range(len(order)):
        values = block(n).astype(jnp.float32)
        normed[n] = (values * scale * gain[pl.ds(slots[n], 1), :]).astype(jnp.bfloat16)
    logits = jnp.zeros((tok, vocab), jnp.float32)
    for n in range(len(order)):
        copies[n].wait()
        logits = logits + lax.dot_general(
            normed[n], weights[n], (((1,), (1,)), ((), ())), preferred_element_type=jnp.float32
        )
    size = sections * rows
    codes = [
        pieces[1][x * ys * size : x * ys * size + size, half:].astype(jnp.float32) for x in range(dps)
    ]
    codes = codes[0] if dps == 1 else jnp.concatenate(codes, axis=0)
    ids = jnp.zeros((tok, 1), jnp.float32)
    for digit in range(DIGITS):
        ids = ids * BASE + codes[:, digit : digit + 1]
    column = device * vocab + lax.broadcasted_iota(jnp.int32, (tok, vocab), 1)
    row_max = jnp.max(logits, axis=1, keepdims=True)
    sums = jnp.sum(jnp.exp(logits - row_max), axis=1, keepdims=True)
    chosen = jnp.sum(
        jnp.where(ids.astype(jnp.int32) == column, logits, 0.0), axis=1, keepdims=True
    )
    row = lax.broadcasted_iota(jnp.int32, (tok, tok), 0)
    place = lax.broadcasted_iota(jnp.int32, (tok, tok), 1)
    from_x = lax.rem(dp + dps - row // (sections * rows), dps)
    from_z = lax.rem(section + sections - lax.rem(row // rows, sections), sections)
    match = (from_z * dps + from_x) * rows + lax.rem(row, rows) == place
    devices = out.shape[0]
    for n, value in enumerate((row_max, sums, chosen)):
        line = jnp.sum(jnp.where(match, value, 0.0), axis=0, keepdims=True)
        out[:, n * tok : (n + 1) * tok] = jnp.broadcast_to(line, (devices, tok))
    out[:, 3 * tok :] = jnp.broadcast_to(extra[...], (devices, extra.shape[1]))


def loss_kernel(own, where, stats, token_logp, group_loss, group_count):
    devices = stats.shape[0]
    tok = devices * own
    maxima = stats[:, :tok]
    row_max = jnp.max(maxima, axis=0, keepdims=True)
    totals = jnp.sum(stats[:, tok : 2 * tok] * jnp.exp(maxima - row_max), axis=0, keepdims=True)
    chosen = jnp.sum(stats[:, 2 * tok : 3 * tok], axis=0, keepdims=True)
    logprob = chosen - (row_max + jnp.log(totals))
    extra = stats[:, 3 * tok :]
    row = lax.broadcasted_iota(jnp.int32, (devices, tok), 0)
    lane = lax.broadcasted_iota(jnp.int32, (devices, tok), 1)
    mine = lax.broadcasted_iota(jnp.int32, (devices, 1), 0) == where[4]
    group_lane = lax.broadcasted_iota(jnp.int32, (devices, GROUPS), 1).astype(jnp.float32)
    own_lane = lax.broadcasted_iota(jnp.int32, (1, own), 1)
    loss_sum = jnp.zeros((devices, GROUPS), jnp.float32)
    count_sum = jnp.zeros((devices, GROUPS), jnp.float32)
    kept = jnp.zeros((1, own), jnp.float32)
    for j in range(own):
        value = jnp.sum(jnp.where(lane == row * own + j, logprob, 0.0), axis=1, keepdims=True)
        old, ref, advantage, weight, live, group = (
            extra[:, j * FIELDS + f : j * FIELDS + f + 1] for f in range(FIELDS)
        )
        losses = token_loss(value, old, ref, advantage, weight)
        hit = group == group_lane
        loss_sum = loss_sum + jnp.where(hit, losses, 0.0)
        count_sum = count_sum + jnp.where(hit, weight, 0.0)
        result = jnp.sum(jnp.where(mine & (live > 0.0), value, 0.0), axis=0, keepdims=True)
        kept = jnp.where(own_lane == j, result, kept)
    token_logp[...] = kept
    group_loss[...] = jnp.sum(loss_sum, axis=0, keepdims=True)
    group_count[...] = jnp.sum(count_sum, axis=0, keepdims=True)


def local(
    hidden,
    norm_gain,
    head_weight,
    token_ids,
    resp_len,
    group_of,
    loss_mask,
    old_logp,
    ref_logp,
    advantage,
):
    rows, width = hidden.shape
    half = width // 2
    sections, dps, tensors = (lax.axis_size(a) for a in ALL)
    devices = sections * dps * tensors
    cores = 2 if tensors % 2 == 0 else 1
    ys = tensors // cores
    tensor_idx = lax.axis_index("tensor")
    device = lax.axis_index(ALL)
    own = loss_mask.shape[0]

    seq_count = resp_len.shape[1]
    window = rows // seq_count
    own_row = tensor_idx * own + jnp.arange(own, dtype=jnp.int32)
    member = (own_row // window)[:, None] == jnp.arange(seq_count, dtype=jnp.int32)[None, :]
    length = jnp.sum(jnp.where(member, resp_len, 0), axis=1)
    group = jnp.sum(jnp.where(member, group_of, 0), axis=1)
    live = (own_row % window >= window - length).astype(jnp.float32)
    weight = live * loss_mask.astype(jnp.float32)
    fields = jnp.stack(
        [old_logp, ref_logp, advantage, weight, live, group.astype(jnp.float32)], axis=1
    ).reshape(1, own * FIELDS)
    extra_width = -(-own * FIELDS // LANES) * LANES
    extra = jnp.pad(fields, ((0, 0), (0, extra_width - own * FIELDS)))

    digits = jnp.stack(
        [token_ids // BASE ** (DIGITS - 1 - d) % BASE for d in range(DIGITS)], axis=1
    ).astype(jnp.bfloat16)
    codes = jnp.pad(digits, ((0, 0), (0, LANES - DIGITS)))

    first = hidden[:, :half]
    second = jnp.concatenate([hidden[:, half:], codes], axis=1)
    first = spread(first, "section", sections)
    second = spread(second, "section", sections)
    first = spread(first, "dp", dps)
    second = spread(second, "tensor", ys, cores)
    first = spread(first, "tensor", ys, cores)
    second = spread(second, "dp", dps)
    pieces = [first, second]
    for k in range(1, cores):
        pairs = [(i, i // cores * cores + (i + k) % cores) for i in range(tensors)]
        pieces += [lax.ppermute(first, "tensor", pairs), lax.ppermute(second, "tensor", pairs)]

    where = jnp.stack(
        [
            lax.axis_index("section"),
            lax.axis_index("dp"),
            tensor_idx // cores,
            tensor_idx % cores,
            device,
        ]
    ).astype(jnp.int32)
    tok = sections * dps * rows
    blocks = 2 * tensors
    vocab = head_weight.shape[0]
    vmem = pl.BlockSpec(memory_space=pltpu.VMEM)
    smem = pl.BlockSpec(memory_space=pltpu.SMEM)
    stats = pl.pallas_call(
        lambda *refs: head_kernel((rows, half, sections, dps, ys, cores), *refs),
        out_shape=jax.ShapeDtypeStruct((devices, 3 * tok + extra_width), jnp.float32),
        in_specs=[smem] + [vmem] * (len(pieces) + 2) + [pl.BlockSpec(memory_space=pl.ANY)],
        out_specs=vmem,
        scratch_shapes=[
            pltpu.VMEM((blocks, vocab, half), jnp.bfloat16),
            pltpu.VMEM((blocks, tok, half), jnp.bfloat16),
            pltpu.SemaphoreType.DMA((blocks,)),
        ],
    )(where, *pieces, norm_gain.reshape(blocks, half), extra, head_weight)
    stats = lax.all_to_all(stats, ALL, 0, 0, tiled=True)
    token_logp, group_loss, group_count = pl.pallas_call(
        lambda *refs: loss_kernel(own, *refs),
        out_shape=[
            jax.ShapeDtypeStruct((1, own), jnp.float32),
            jax.ShapeDtypeStruct((1, GROUPS), jnp.float32),
            jax.ShapeDtypeStruct((1, GROUPS), jnp.float32),
        ],
        in_specs=[smem, vmem],
        out_specs=[vmem] * 3,
    )(where, stats)
    return (token_logp[0], group_loss[0], group_count[0])


def solution(mesh):
    return jax.shard_map(
        local,
        mesh=mesh,
        in_specs=(
            P(("section", "dp"), "tensor"),
            P(),
            P(("section", "dp", "tensor"), None),
            P(("section", "dp")),
            P(("section", "dp"), None),
            P(("section", "dp"), None),
            P(("section", "dp", "tensor")),
            P(("section", "dp", "tensor")),
            P(("section", "dp", "tensor")),
            P(("section", "dp", "tensor")),
        ),
        out_specs=(P(("section", "dp", "tensor")), P(), P()),
        check_vma=False,
    )
```

time: 172 us -> 61.6 us (0.36)
  blocking collectives: 106 us -> 11.9 us
  waiting for transfers between devices: 33.3 us -> 8.53 us
  starting transfers between devices: 0.04 us -> 17.4 us
  between operations: 14.8 us -> 0.76 us
  Pallas kernels: 0 us -> 10.5 us
  matrix products: 6.78 us -> 0 us
  local copies, waits for them, and re-layouts: 5.15 us -> 9.69 us
  other arithmetic: 5.37 us -> 2.4 us
    unnamed x2 -> x0, blocking collectives: 51.3 us -> none
    psum x2 -> x0, blocking collectives: 48.4 us -> none  [the longest x1 40 us: local(): lax.psum((jnp.sum(group_hit * losses[:, None], axis=0), jnp.sum(group_hit...]
    all_gather x1 -> x0, waiting for transfers between devices: 33.2 us -> none  [local(): piece_rows = lax.all_gather(gathered, ('section', 'dp'), axis=0, tiled=True)]
    ppermute x0 -> x12, starting transfers between devices: none -> 17.4 us  [the longest x10 17.3 us: spread(): blocks.append(lax.ppermute(x, axis, pairs))]
    all_to_all x0 -> x1, blocking collectives: none -> 11.9 us  [local(): stats = lax.all_to_all(stats, ALL, 0, 0, tiled=True)]
    pallas_call x0 -> x2, Pallas kernels: none -> 10.5 us  [the longest x1 8.75 us: local(): pl.pallas_call(lambda *refs: head_kernel((rows, half, sections, dps, ys,...]
    ppermute x0 -> x12, waiting for transfers between devices: none -> 8.53 us  [the longest x10 8.53 us: spread(): blocks.append(lax.ppermute(x, axis, pairs))]
    dot_general x1 -> x0, matrix products: 6.78 us -> none  [local(): jnp.einsum('rd,vd->rv', piece_rows, head_weight, preferred_element_type=j...]
  transfers between devices with their start and end apart: 1 -> 12, of which waited for: 1 -> 7; matrix products, arithmetic and copies ran while one was open for 2% -> 13% of each run, Pallas kernels for 0% -> 0%
where the time goes in v1:
time: 61.6 us; the launch traced here: 61.2 us
  starting transfers between devices  17.4 us (28%)
  blocking collectives  11.9 us (19%)
  Pallas kernels  10.5 us (17%)
  local copies, waits for them, and re-layouts  9.69 us (16%)
  waiting for transfers between devices  8.53 us (14%)
  other arithmetic  2.4 us (4%)
  between operations  0.76 us (1%)
    ppermute x10, starting transfers between devices, spread(): blocks.append(lax.ppermute(x, axis, pairs))  17.3 us
    all_to_all x1, blocking collectives, local(): stats = lax.all_to_all(stats, ALL, 0, 0, tiled=True)  11.9 us
    pallas_call x1, Pallas kernels, local(): pl.pallas_call(lambda *refs: head_kernel((rows, half, sections, dps, ys,...  8.75 us
    ppermute x10, waiting for transfers between devices, spread(): blocks.append(lax.ppermute(x, axis, pairs))  8.53 us
    another operation x5, local copies, waits for them, and re-layouts, local(): jnp.stack([old_logp, ref_logp, advantage, weight, live, group.astype(jnp....  2.41 us
    unnamed x15, local copies, waits for them, and re-layouts  2.26 us
    pallas_call x1, Pallas kernels, local(): pl.pallas_call(lambda *refs: loss_kernel(own, *refs), out_shape=[jax.Shap...  1.74 us
    reshape x1, local copies, waits for them, and re-layouts, local(): norm_gain.reshape(blocks, half)  1.47 us
  transfers between devices with their start and end apart: 12, of which 7 were waited for; matrix products, arithmetic and copies ran while one was open for 13% of the time, Pallas kernels for 0%

profile of v1, /device:TPU:0, one launch (start us, length us, event | category | flops | bytes accessed | tf_op | source)
XLA Modules:
  0.0 61.2 jit_solution(8959706095422452233)
XLA Ops:
  0.6 0.8 %fusion.15 = (bf16[8,2048]{1,0:T(8,128)(2,1)S(1)}, bf16[64,2048]{1,0:T(8,128)(2,1)S(1)}, bf16[128,2048]{1,0:T(8,128)(2,1)S(1)}, bf16[8,2048]{1,0:T(8,128)(2,1)S(1)}) fusion(bf16[8,4096]{1,0:T(8,128)(2,1)} %param.10), kind=kLoop, calls=%fused_computation.72 | loop fusion | bytes 196608 | tf_op jit(solution)/shard_map/slice | solution.py:200
  1.4 3.1 %collective-permute-start = (bf16[8,2048]{1,0:T(8,128)(2,1)S(1)}, bf16[8,2048]{1,0:T(8,128)(2,1)S(1)}, u32[]{:S(2)}, u32[]{:S(2)}) collective-permute-start(bf16[8,2048]{1,0:T(8,128)(2,1)S(1)} %get-tuple-element.18), channel_id=1, source_target_pairs={{0,8},{8,16},{16,24},{24,0},{1,9},{9,17},{17,25},{25,1},{2,10},{10... | collective-permute-start | bytes 98312 | tf_op jit(solution)/shard_map/ppermute | solution.py:43
  4.5 2.6 %collective-permute-start.1 = (bf16[8,2048]{1,0:T(8,128)(2,1)S(1)}, bf16[8,2048]{1,0:T(8,128)(2,1)S(1)}, u32[]{:S(2)}, u32[]{:S(2)}) collective-permute-start(bf16[8,2048]{1,0:T(8,128)(2,1)S(1)} %get-tuple-element.18), channel_id=1, source_target_pairs={{0,16},{8,24},{16,0},{24,8},{1,17},{9,25},{17,1},{25,9},{2,18},{10... | collective-permute-start | bytes 98312 | tf_op jit(solution)/shard_map/ppermute | solution.py:43
  7.1 1.3 %collective-permute-start.2 = (bf16[8,2048]{1,0:T(8,128)(2,1)S(1)}, bf16[8,2048]{1,0:T(8,128)(2,1)S(1)}, u32[]{:S(2)}, u32[]{:S(2)}) collective-permute-start(bf16[8,2048]{1,0:T(8,128)(2,1)S(1)} %get-tuple-element.18), channel_id=1, source_target_pairs={{0,24},{8,0},{16,8},{24,16},{1,25},{9,1},{17,9},{25,17},{2,26},{10... | collective-permute-start | bytes 98312 | tf_op jit(solution)/shard_map/ppermute | solution.py:43
  8.5 0.7 %fusion.6 = (bf16[8,1]{0,1:T(2,128)(2,1)S(1)}, bf16[8,1]{0,1:T(2,128)(2,1)S(1)}, bf16[8,1]{0,1:T(2,128)(2,1)S(1)}) fusion(s32[8]{0:T(128)} %param.13), kind=kLoop, calls=%fused_computation.60 | loop fusion | flops 432 | bytes 80 | tf_op jit(solution)/shard_map/stack | solution.py:194
  9.1 0.1 copy.29
  9.2 0.1 copy.28
  9.3 0.1 copy.27
  9.4 0.1 fusion.4
  9.5 0.7 %collective-permute-start.5 = (bf16[8,2176]{1,0:T(8,128)(2,1)S(1)}, bf16[8,2176]{1,0:T(8,128)(2,1)S(1)}, u32[]{:S(2)}, u32[]{:S(2)}) collective-permute-start(bf16[8,2176]{1,0:T(8,128)(2,1)S(1)} %get-tuple-element.27), channel_id=1, source_target_pairs={{0,8},{8,16},{16,24},{24,0},{1,9},{9,17},{17,25},{25,1},{2,10},{10... | collective-permute-start | bytes 104456 | tf_op jit(solution)/shard_map/ppermute | solution.py:43
  10.2 0.3 collective-permute-start.6
  10.6 0.0 collective-permute-done
  10.6 2.9 %collective-permute-start.7 = (bf16[8,2176]{1,0:T(8,128)(2,1)S(1)}, bf16[8,2176]{1,0:T(8,128)(2,1)S(1)}, u32[]{:S(2)}, u32[]{:S(2)}) collective-permute-start(bf16[8,2176]{1,0:T(8,128)(2,1)S(1)} %get-tuple-element.27), channel_id=1, source_target_pairs={{0,24},{8,0},{16,8},{24,16},{1,25},{9,1},{17,9},{25,17},{2,26},{10... | collective-permute-start | bytes 104456 | tf_op jit(solution)/shard_map/ppermute | solution.py:43
  13.5 0.0 collective-permute-done.1
  13.5 0.0 collective-permute-done.2
  13.5 1.6 %collective-permute-start.3 = (bf16[32,2048]{1,0:T(8,128)(2,1)S(1)}, bf16[32,2048]{1,0:T(8,128)(2,1)S(1)}, u32[]{:S(2)}, u32[]{:S(2)}) collective-permute-start(bf16[32,2048]{1,0:T(8,128)(2,1)S(1)} %pad_maximum_fusion.1), channel_id=1, source_target_pairs={{0,4},{4,0},{1,5},{5,1},{2,6},{6,2},{3,7},{7,3},{8,12},{12,8},{9,1... | collective-permute-start | bytes 393224 | tf_op jit(solution)/shard_map/ppermute | solution.py:43
  15.1 0.3 collective-permute-done.5
  15.4 0.7 %collective-permute-done.6 = bf16[8,2176]{1,0:T(8,128)(2,1)S(1)} collective-permute-done((bf16[8,2176]{1,0:T(8,128)(2,1)S(1)}, bf16[8,2176]{1,0:T(8,128)(2,1)S(1)}, u32[]{:S(2)}, u32[]{:S(2)}) %collective-permute-start.6) | collective-permute-done | bytes 34848 | tf_op jit(solution)/shard_map/ppermute | solution.py:43
  16.1 0.1 collective-permute-done.7
  16.2 1.6 %collective-permute-start.8 = (bf16[32,2176]{1,0:T(8,128)(2,1)S(1)}, bf16[32,2176]{1,0:T(8,128)(2,1)S(1)}, u32[]{:S(2)}, u32[]{:S(2)}) collective-permute-start(bf16[32,2176]{1,0:T(8,128)(2,1)S(1)} %pad_maximum_fusion), channel_id=1, source_target_pairs={{0,2},{1,3},{2,0},{3,1},{4,6},{5,7},{6,4},{7,5},{8,10},{9,11},{10,... | collective-permute-start | bytes 417800 | tf_op jit(solution)/shard_map/ppermute | solution.py:43
  17.8 0.7 %collective-permute-done.3 = bf16[32,2048]{1,0:T(8,128)(2,1)S(1)} collective-permute-done((bf16[32,2048]{1,0:T(8,128)(2,1)S(1)}, bf16[32,2048]{1,0:T(8,128)(2,1)S(1)}, u32[]{:S(2)}, u32[]{:S(2)}) %collective-permute-start.3) | collective-permute-done | bytes 131104 | tf_op jit(solution)/shard_map/ppermute | solution.py:43
  18.5 1.6 %collective-permute-start.4 = (bf16[64,2048]{1,0:T(8,128)(2,1)S(1)}, bf16[64,2048]{1,0:T(8,128)(2,1)S(1)}, u32[]{:S(2)}, u32[]{:S(2)}) collective-permute-start(bf16[64,2048]{1,0:T(8,128)(2,1)S(1)} %get-tuple-element.13), channel_id=1, source_target_pairs={{0,2},{1,3},{2,0},{3,1},{4,6},{5,7},{6,4},{7,5},{8,10},{9,11},{10,... | collective-permute-start | bytes 786440 | tf_op jit(solution)/shard_map/ppermute | solution.py:43
  20.1 2.6 %collective-permute-done.8 = bf16[32,2176]{1,0:T(8,128)(2,1)S(1)} collective-permute-done((bf16[32,2176]{1,0:T(8,128)(2,1)S(1)}, bf16[32,2176]{1,0:T(8,128)(2,1)S(1)}, u32[]{:S(2)}, u32[]{:S(2)}) %collective-permute-start.8) | collective-permute-done | bytes 139296 | tf_op jit(solution)/shard_map/ppermute | solution.py:43
  22.8 1.6 %collective-permute-start.9 = (bf16[64,2176]{1,0:T(8,128)(2,1)S(1)}, bf16[64,2176]{1,0:T(8,128)(2,1)S(1)}, u32[]{:S(2)}, u32[]{:S(2)}) collective-permute-start(bf16[64,2176]{1,0:T(8,128)(2,1)S(1)} %get-tuple-element.11), channel_id=1, source_target_pairs={{0,4},{4,0},{1,5},{5,1},{2,6},{6,2},{3,7},{7,3},{8,12},{12,8},{9,1... | collective-permute-start | bytes 835592 | tf_op jit(solution)/shard_map/ppermute | solution.py:43
  24.4 0.9 %select_reduce_fusion = (s32[2]{0:T(128)S(1)}, s32[2]{0:T(128)S(1)}) fusion(s32[2]{0:T(128)} %bitcast.31, s32[2]{0:T(128)S(1)} %and_select_fusion.1, s32[2]{0:T(128)} %bitcast.32), kind=kLoop, calls=%fused_computation.51 | loop fusion | flops 16 | bytes 40 | tf_op jit(solution)/shard_map/reduce_sum | solution.py:185
  25.2 0.7 %collective-permute-done.4 = bf16[64,2048]{1,0:T(8,128)(2,1)S(1)} collective-permute-done((bf16[64,2048]{1,0:T(8,128)(2,1)S(1)}, bf16[64,2048]{1,0:T(8,128)(2,1)S(1)}, u32[]{:S(2)}, u32[]{:S(2)}) %collective-permute-start.4) | collective-permute-done | bytes 262176 | tf_op jit(solution)/shard_map/ppermute | solution.py:43
  25.9 0.1 collective-permute-start.10
  26.0 3.4 %collective-permute-done.9 = bf16[64,2176]{1,0:T(8,128)(2,1)S(1)} collective-permute-done((bf16[64,2176]{1,0:T(8,128)(2,1)S(1)}, bf16[64,2176]{1,0:T(8,128)(2,1)S(1)}, u32[]{:S(2)}, u32[]{:S(2)}) %collective-permute-start.9) | collective-permute-done | bytes 278560 | tf_op jit(solution)/shard_map/ppermute | solution.py:43
  29.5 0.1 collective-permute-start.11
  29.5 0.7 %fusion.14 = f32[2,1]{0,1:T(1,128)S(1)} fusion(s32[2]{0:T(128)} %param.16, s32[2]{0:T(128)S(1)} %get-tuple-element.10, s32[]{:T(128)S(6)} %mul.14), kind=kLoop, calls=%fused_computation.70 | loop fusion | flops 32 | bytes 28 | tf_op jit(solution)/shard_map/stack | solution.py:188
  30.2 1.5 %reshape.94.refs_5_ = f32[8,2048]{1,0:T(8,128)} reshape(f32[16384]{0:T(1024)} %param.11) | data formatting | bytes 131072 | tf_op jit(solution)/shard_map/reshape | solution.py:236
  31.7 0.7 %copy.30 = f32[2,1]{1,0:T(2,128)S(1)} copy(f32[2,1]{0,1:T(1,128)} %bitcast.33) | data formatting | bytes 16 | tf_op jit(solution)/shard_map/stack | solution.py:188
  32.5 0.7 %copy.31 = f32[2,1]{1,0:T(2,128)S(1)} copy(f32[2,1]{0,1:T(1,128)} %bitcast.34) | data formatting | bytes 16 | tf_op jit(solution)/shard_map/stack | solution.py:188
  33.2 0.7 %copy.32 = f32[2,1]{1,0:T(2,128)S(1)} copy(f32[2,1]{0,1:T(1,128)} %bitcast.35) | data formatting | bytes 16 | tf_op jit(solution)/shard_map/stack | solution.py:188
  33.9 0.1 copy.33
  34.0 0.1 copy.34
  34.1 0.1 copy.35
  34.2 0.1 stack.65
  34.3 0.1 reshape.95
  34.4 0.6 pad.9.refs_6_
  35.0 0.7 %stack.56.refs_0_ = s32[5]{0:T(128)} concatenate(s32[1]{0:T(128)} %bitcast, s32[1]{0:T(128)} %bitcast.1, s32[1]{0:T(128)} %bitcast.2, s32[1]{0:T(128)} %bitcast.3, s32[1]{0:T(128)} %bitcast.4), dimensions={0} | concatenate | bytes 40 | tf_op jit(solution)/shard_map/stack | solution.py:212
  35.7 0.8 %copy-done.3 = bf16[128,2048]{1,0:T(8,128)(2,1)} copy-done((bf16[128,2048]{1,0:T(8,128)(2,1)}, bf16[128,2048]{1,0:T(8,128)(2,1)S(1)}, u32[]{:S(2)}) %copy-start.3) | copy-done | bytes 524312
  36.5 0.8 %copy-done.2 = bf16[128,2176]{1,0:T(8,128)(2,1)} copy-done((bf16[128,2176]{1,0:T(8,128)(2,1)}, bf16[128,2176]{1,0:T(8,128)(2,1)S(1)}, u32[]{:S(2)}) %copy-start.2) | copy-done | bytes 557080
  37.3 8.8 %shard_map.121 = f32[32,320]{1,0:T(8,128)} custom-call(s32[5]{0:T(128)} %stack.56.refs_0_, bf16[128,2048]{1,0:T(8,128)(2,1)} %copy-done.1, bf16[128,2176]{1,0:T(8,128)(2,1)} %copy-done, bf16[128,2048]{1,0:T(8,128)(2,1)} %copy-done.3, bf16[128,2176]{1,0:T(8,128)(2,1)} %copy-done.2, f32[8,2048]{1,0:T(8,128)} %reshape.94.refs_5_, f32[1,128]{1,0:T(1,128)} %pad.9.refs_6_, ...), custom_call_target="tpu_custom_call" | custom-call | tf_op jit(solution)/shard_map/pallas_call | solution.py:226
  46.1 0.9 %copy.36 = f32[32,1,320]{2,1,0:T(1,128)S(1)} copy(f32[32,1,320]{2,0,1:T(8,128)} %bitcast.29) | data formatting | bytes 81920 | tf_op jit(solution)/shard_map/all_to_all | solution.py:237
  46.9 11.9 %all_to_all.11 = f32[32,1,320]{2,1,0:T(1,128)S(1)} all-to-all(f32[32,1,320]{2,1,0:T(1,128)S(1)} %copy.36), channel_id=1, replica_groups=mesh['section'=4,'dp'=2,'tensor'=4] {'section','dp','tensor'}, dimensions={0} | all-to-all | bytes 81920 | tf_op jit(solution)/shard_map/all_to_all | solution.py:237
  58.8 0.6 %copy.39 = f32[32,1,320]{2,0,1:T(8,128)} copy(f32[32,1,320]{2,1,0:T(1,128)S(1)} %all_to_all.11) | data formatting | bytes 81920
  59.4 1.7 %shard_map.122 = (f32[1,2]{1,0:T(1,128)}, f32[1,8]{1,0:T(1,128)}, f32[1,8]{1,0:T(1,128)}) custom-call(s32[5]{0:T(128)} %stack.56.refs_0_, f32[32,320]{1,0:T(8,128)} %bitcast.30), custom_call_target="tpu_custom_call" | custom-call | tf_op jit(solution)/shard_map/pallas_call | solution.py:238
  (24 shorter events, 0.2 us)
Async XLA Ops:
  1.4 9.2 %collective-permute-start = (bf16[8,2048]{1,0:T(8,128)(2,1)S(1)}, bf16[8,2048]{1,0:T(8,128)(2,1)S(1)}, u32[]{:S(2)}, u32[]{:S(2)}) collective-permute-start(bf16[8,2048]{1,0:T(8,128)(2,1)S(1)} %get-tuple-element.18), channel_id=1, source_target_pairs={{0,8},{8,16},{16,24},{24,0},{1,9},{9,17},{17,25},{25,1},{2,10},{10... | collective-permute-start | bytes 98312 | tf_op jit(solution)/shard_map/ppermute | solution.py:43
  4.5 9.0 %collective-permute-start.1 = (bf16[8,2048]{1,0:T(8,128)(2,1)S(1)}, bf16[8,2048]{1,0:T(8,128)(2,1)S(1)}, u32[]{:S(2)}, u32[]{:S(2)}) collective-permute-start(bf16[8,2048]{1,0:T(8,128)(2,1)S(1)} %get-tuple-element.18), channel_id=1, source_target_pairs={{0,16},{8,24},{16,0},{24,8},{1,17},{9,25},{17,1},{25,9},{2,18},{10... | collective-permute-start | bytes 98312 | tf_op jit(solution)/shard_map/ppermute | solution.py:43
  7.1 6.4 %collective-permute-start.2 = (bf16[8,2048]{1,0:T(8,128)(2,1)S(1)}, bf16[8,2048]{1,0:T(8,128)(2,1)S(1)}, u32[]{:S(2)}, u32[]{:S(2)}) collective-permute-start(bf16[8,2048]{1,0:T(8,128)(2,1)S(1)} %get-tuple-element.18), channel_id=1, source_target_pairs={{0,24},{8,0},{16,8},{24,16},{1,25},{9,1},{17,9},{25,17},{2,26},{10... | collective-permute-start | bytes 98312 | tf_op jit(solution)/shard_map/ppermute | solution.py:43
  9.5 5.9 %collective-permute-start.5 = (bf16[8,2176]{1,0:T(8,128)(2,1)S(1)}, bf16[8,2176]{1,0:T(8,128)(2,1)S(1)}, u32[]{:S(2)}, u32[]{:S(2)}) collective-permute-start(bf16[8,2176]{1,0:T(8,128)(2,1)S(1)} %get-tuple-element.27), channel_id=1, source_target_pairs={{0,8},{8,16},{16,24},{24,0},{1,9},{9,17},{17,25},{25,1},{2,10},{10... | collective-permute-start | bytes 104456 | tf_op jit(solution)/shard_map/ppermute | solution.py:43
  10.2 5.8 %collective-permute-start.6 = (bf16[8,2176]{1,0:T(8,128)(2,1)S(1)}, bf16[8,2176]{1,0:T(8,128)(2,1)S(1)}, u32[]{:S(2)}, u32[]{:S(2)}) collective-permute-start(bf16[8,2176]{1,0:T(8,128)(2,1)S(1)} %get-tuple-element.27), channel_id=1, source_target_pairs={{0,16},{8,24},{16,0},{24,8},{1,17},{9,25},{17,1},{25,9},{2,18},{10... | collective-permute-start | bytes 104456 | tf_op jit(solution)/shard_map/ppermute | solution.py:43
  10.6 5.6 %collective-permute-start.7 = (bf16[8,2176]{1,0:T(8,128)(2,1)S(1)}, bf16[8,2176]{1,0:T(8,128)(2,1)S(1)}, u32[]{:S(2)}, u32[]{:S(2)}) collective-permute-start(bf16[8,2176]{1,0:T(8,128)(2,1)S(1)} %get-tuple-element.27), channel_id=1, source_target_pairs={{0,24},{8,0},{16,8},{24,16},{1,25},{9,1},{17,9},{25,17},{2,26},{10... | collective-permute-start | bytes 104456 | tf_op jit(solution)/shard_map/ppermute | solution.py:43
  13.5 5.0 %collective-permute-start.3 = (bf16[32,2048]{1,0:T(8,128)(2,1)S(1)}, bf16[32,2048]{1,0:T(8,128)(2,1)S(1)}, u32[]{:S(2)}, u32[]{:S(2)}) collective-permute-start(bf16[32,2048]{1,0:T(8,128)(2,1)S(1)} %pad_maximum_fusion.1), channel_id=1, source_target_pairs={{0,4},{4,0},{1,5},{5,1},{2,6},{6,2},{3,7},{7,3},{8,12},{12,8},{9,1... | collective-permute-start | bytes 393224 | tf_op jit(solution)/shard_map/ppermute | solution.py:43
  16.2 6.6 %collective-permute-start.8 = (bf16[32,2176]{1,0:T(8,128)(2,1)S(1)}, bf16[32,2176]{1,0:T(8,128)(2,1)S(1)}, u32[]{:S(2)}, u32[]{:S(2)}) collective-permute-start(bf16[32,2176]{1,0:T(8,128)(2,1)S(1)} %pad_maximum_fusion), channel_id=1, source_target_pairs={{0,2},{1,3},{2,0},{3,1},{4,6},{5,7},{6,4},{7,5},{8,10},{9,11},{10,... | collective-permute-start | bytes 417800 | tf_op jit(solution)/shard_map/ppermute | solution.py:43
  18.5 7.3 %collective-permute-start.4 = (bf16[64,2048]{1,0:T(8,128)(2,1)S(1)}, bf16[64,2048]{1,0:T(8,128)(2,1)S(1)}, u32[]{:S(2)}, u32[]{:S(2)}) collective-permute-start(bf16[64,2048]{1,0:T(8,128)(2,1)S(1)} %get-tuple-element.13), channel_id=1, source_target_pairs={{0,2},{1,3},{2,0},{3,1},{4,6},{5,7},{6,4},{7,5},{8,10},{9,11},{10,... | collective-permute-start | bytes 786440 | tf_op jit(solution)/shard_map/ppermute | solution.py:43
  22.8 6.6 %collective-permute-start.9 = (bf16[64,2176]{1,0:T(8,128)(2,1)S(1)}, bf16[64,2176]{1,0:T(8,128)(2,1)S(1)}, u32[]{:S(2)}, u32[]{:S(2)}) collective-permute-start(bf16[64,2176]{1,0:T(8,128)(2,1)S(1)} %get-tuple-element.11), channel_id=1, source_target_pairs={{0,4},{4,0},{1,5},{5,1},{2,6},{6,2},{3,7},{7,3},{8,12},{12,8},{9,1... | collective-permute-start | bytes 835592 | tf_op jit(solution)/shard_map/ppermute | solution.py:43
  25.9 9.8 %copy-start.1 = (bf16[128,2048]{1,0:T(8,128)(2,1)}, bf16[128,2048]{1,0:T(8,128)(2,1)S(1)}, u32[]{:S(2)}) copy-start(bf16[128,2048]{1,0:T(8,128)(2,1)S(1)} %constant_dynamic-update-slice_fusion.5.refs_1_) | copy-start | bytes 1572868
  25.9 9.8 %collective-permute-start.10 = (bf16[128,2048]{1,0:T(8,128)(2,1)S(1)}, bf16[128,2048]{1,0:T(8,128)(2,1)S(1)}, u32[]{:S(2)}, u32[]{:S(2)}) collective-permute-start(bf16[128,2048]{1,0:T(8,128)(2,1)S(1)} %constant_dynamic-update-slice_fusion.5.refs_1_), channel_id=1, source_target_pairs={{0,1},{1,0},{2,3},{3,2},{4,5},{5,4},{6,7},{7,6},{8,9},{9,8},{10,11... | collective-permute-start | bytes 1572872 | tf_op jit(solution)/shard_map/ppermute | solution.py:210
  29.4 6.3 %copy-start = (bf16[128,2176]{1,0:T(8,128)(2,1)}, bf16[128,2176]{1,0:T(8,128)(2,1)S(1)}, u32[]{:S(2)}) copy-start(bf16[128,2176]{1,0:T(8,128)(2,1)S(1)} %constant_dynamic-update-slice_fusion.16.refs_2_) | copy-start | bytes 1671172
  29.5 6.2 %collective-permute-start.11 = (bf16[128,2176]{1,0:T(8,128)(2,1)S(1)}, bf16[128,2176]{1,0:T(8,128)(2,1)S(1)}, u32[]{:S(2)}, u32[]{:S(2)}) collective-permute-start(bf16[128,2176]{1,0:T(8,128)(2,1)S(1)} %constant_dynamic-update-slice_fusion.16.refs_2_), channel_id=1, source_target_pairs={{0,1},{1,0},{2,3},{3,2},{4,5},{5,4},{6,7},{7,6},{8,9},{9,8},{10,11... | collective-permute-start | bytes 1671176 | tf_op jit(solution)/shard_map/ppermute | solution.py:210
  35.7 0.8 %copy-start.3 = (bf16[128,2048]{1,0:T(8,128)(2,1)}, bf16[128,2048]{1,0:T(8,128)(2,1)S(1)}, u32[]{:S(2)}) copy-start(bf16[128,2048]{1,0:T(8,128)(2,1)S(1)} %collective-permute-done.10.refs_3_) | copy-start | bytes 1572868
  36.5 0.8 %copy-start.2 = (bf16[128,2176]{1,0:T(8,128)(2,1)}, bf16[128,2176]{1,0:T(8,128)(2,1)S(1)}, u32[]{:S(2)}) copy-start(bf16[128,2176]{1,0:T(8,128)(2,1)S(1)} %collective-permute-done.11.refs_4_) | copy-start | bytes 1671172

commit v2 on v1

--- a/solution.py
+++ b/solution.py
@@ -9,7 +9,7 @@
 LANES = 128
 FIELDS = 6
 DIGITS = 3
-BASE = 256
+BITS = 8
 
 epsilon = 1e-05
 clip_range = 0.2
@@ -103,7 +103,7 @@
     codes = codes[0] if dps == 1 else jnp.concatenate(codes, axis=0)
     ids = jnp.zeros((tok, 1), jnp.float32)
     for digit in range(DIGITS):
-        ids = ids * BASE + codes[:, digit : digit + 1]
+        ids = ids * 2**BITS + codes[:, digit : digit + 1]
     column = device * vocab + lax.broadcasted_iota(jnp.int32, (tok, vocab), 1)
     row_max = jnp.max(logits, axis=1, keepdims=True)
     sums = jnp.sum(jnp.exp(logits - row_max), axis=1, keepdims=True)
@@ -115,16 +115,18 @@
     from_x = lax.rem(dp + dps - row // (sections * rows), dps)
     from_z = lax.rem(section + sections - lax.rem(row // rows, sections), sections)
     match = (from_z * dps + from_x) * rows + lax.rem(row, rows) == place
-    devices = out.shape[0]
+    lines = []
     for n, value in enumerate((row_max, sums, chosen)):
         line = jnp.sum(jnp.where(match, value, 0.0), axis=0, keepdims=True)
-        out[:, n * tok : (n + 1) * tok] = jnp.broadcast_to(line, (devices, tok))
-    out[:, 3 * tok :] = jnp.broadcast_to(extra[...], (devices, extra.shape[1]))
+        lines.append(line)
+    line = jnp.concatenate(lines + [extra[...]], axis=1)
+    out[...] = jnp.broadcast_to(line[None], out.shape)
 
 
 def loss_kernel(own, where, stats, token_logp, group_loss, group_count):
     devices = stats.shape[0]
     tok = devices * own
+    stats = stats[:, 0, :]
     maxima = stats[:, :tok]
     row_max = jnp.max(maxima, axis=0, keepdims=True)
     totals = jnp.sum(stats[:, tok : 2 * tok] * jnp.exp(maxima - row_max), axis=0, keepdims=True)
@@ -142,7 +144,7 @@
     for j in range(own):
         value = jnp.sum(jnp.where(lane == row * own + j, logprob, 0.0), axis=1, keepdims=True)
         old, ref, advantage, weight, live, group = (
-            extra[:, j * FIELDS + f : j * FIELDS + f + 1] for f in range(FIELDS)
+            extra[:, f * own + j : f * own + j + 1] for f in range(FIELDS)
         )
         losses = token_loss(value, old, ref, advantage, weight)
         hit = group == group_lane
@@ -185,30 +187,25 @@
     group = jnp.sum(jnp.where(member, group_of, 0), axis=1)
     live = (own_row % window >= window - length).astype(jnp.float32)
     weight = live * loss_mask.astype(jnp.float32)
-    fields = jnp.stack(
-        [old_logp, ref_logp, advantage, weight, live, group.astype(jnp.float32)], axis=1
-    ).reshape(1, own * FIELDS)
     extra_width = -(-own * FIELDS // LANES) * LANES
-    extra = jnp.pad(fields, ((0, 0), (0, extra_width - own * FIELDS)))
-
-    digits = jnp.stack(
-        [token_ids // BASE ** (DIGITS - 1 - d) % BASE for d in range(DIGITS)], axis=1
-    ).astype(jnp.bfloat16)
-    codes = jnp.pad(digits, ((0, 0), (0, LANES - DIGITS)))
-
-    first = hidden[:, :half]
-    second = jnp.concatenate([hidden[:, half:], codes], axis=1)
-    first = spread(first, "section", sections)
-    second = spread(second, "section", sections)
+    unused = jnp.zeros((extra_width - own * FIELDS,), jnp.float32)
+    extra = jnp.concatenate(
+        [old_logp, ref_logp, advantage, weight, live, group.astype(jnp.float32), unused]
+    )[None, :]
+
+    digit = jnp.arange(LANES, dtype=jnp.int32)[None, :]
+    shift = BITS * jnp.maximum(DIGITS - 1 - digit, 0)
+    codes = lax.shift_right_logical(
+        jnp.broadcast_to(token_ids[:, None], (rows, LANES)), jnp.broadcast_to(shift, (rows, LANES))
+    )
+    codes = jnp.where(digit < DIGITS, codes & (2**BITS - 1), 0).astype(jnp.bfloat16)
+
+    column = spread(jnp.concatenate([hidden, codes], axis=1), "section", sections)
+    first, second = column[:, :half], column[:, half:]
     first = spread(first, "dp", dps)
     second = spread(second, "tensor", ys, cores)
     first = spread(first, "tensor", ys, cores)
     second = spread(second, "dp", dps)
-    pieces = [first, second]
-    for k in range(1, cores):
-        pairs = [(i, i // cores * cores + (i + k) % cores) for i in range(tensors)]
-        pieces += [lax.ppermute(first, "tensor", pairs), lax.ppermute(second, "tensor", pairs)]
-
     where = jnp.stack(
         [
             lax.axis_index("section"),
@@ -218,14 +215,21 @@
             device,
         ]
     ).astype(jnp.int32)
+    blocks = 2 * tensors
+    gain = norm_gain.reshape(blocks, half)
+    second, gain, extra, where = lax.optimization_barrier((second, gain, extra, where))
+    pieces = [first, second]
+    for k in range(1, cores):
+        pairs = [(i, i // cores * cores + (i + k) % cores) for i in range(tensors)]
+        pieces += [lax.ppermute(first, "tensor", pairs), lax.ppermute(second, "tensor", pairs)]
+
     tok = sections * dps * rows
-    blocks = 2 * tensors
     vocab = head_weight.shape[0]
     vmem = pl.BlockSpec(memory_space=pltpu.VMEM)
     smem = pl.BlockSpec(memory_space=pltpu.SMEM)
     stats = pl.pallas_call(
         lambda *refs: head_kernel((rows, half, sections, dps, ys, cores), *refs),
-        out_shape=jax.ShapeDtypeStruct((devices, 3 * tok + extra_width), jnp.float32),
+        out_shape=jax.ShapeDtypeStruct((devices, 1, 3 * tok + extra_width), jnp.float32),
         in_specs=[smem] + [vmem] * (len(pieces) + 2) + [pl.BlockSpec(memory_space=pl.ANY)],
         out_specs=vmem,
         scratch_shapes=[
@@ -233,8 +237,8 @@
             pltpu.VMEM((blocks, tok, half), jnp.bfloat16),
             pltpu.SemaphoreType.DMA((blocks,)),
         ],
-    )(where, *pieces, norm_gain.reshape(blocks, half), extra, head_weight)
-    stats = lax.all_to_all(stats, ALL, 0, 0, tiled=True)
+    )(where, *pieces, gain, extra, head_weight)
+    stats = lax.all_to_all(stats, ALL, 0, 0)
     token_logp, group_loss, group_count = pl.pallas_call(
         lambda *refs: loss_kernel(own, *refs),
         out_shape=[

time: 61.6 us -> 56.4 us (0.916)
  local copies, waits for them, and re-layouts: 9.69 us -> 3.51 us
  waiting for transfers between devices: 8.53 us -> 13.6 us
  starting transfers between devices: 17.4 us -> 12.5 us
  other arithmetic: 2.4 us -> 4.27 us
  blocking collectives: 11.9 us -> 10.6 us
    ppermute x10 -> x7, starting transfers between devices: 17.3 us -> 12.4 us  [spread(): blocks.append(lax.ppermute(x, axis, pairs))]
    ppermute x10 -> x7, waiting for transfers between devices: 8.53 us -> 11.7 us  [spread(): blocks.append(lax.ppermute(x, axis, pairs))]
    another operation x8 -> x0, local copies, waits for them, and re-layouts: 2.69 us -> none  [the longest x5 2.41 us: local(): jnp.stack([old_logp, ref_logp, advantage, weight, live, group.astype(jnp....]
    ppermute x1, waiting for transfers between devices: 0.01 us -> 1.9 us  [local(): lax.ppermute(first, 'tensor', pairs)]
    another operation x3 -> x0, other arithmetic: 1.46 us -> none  [the longest x2 0.75 us: local(): jnp.stack([token_ids // BASE ** (DIGITS - 1 - d) % BASE for d in range(DI...]
    all_to_all x1, blocking collectives: 11.9 us -> 10.6 us  [local(): stats = lax.all_to_all(stats, ALL, 0, 0)]
    concatenate x2 -> x5, other arithmetic: 0.02 us -> 0.98 us  [spread(): return jnp.concatenate(blocks, axis=0)]
    reshape x2 -> x1, local copies, waits for them, and re-layouts: 1.56 us -> 0.64 us  [local(): gain = norm_gain.reshape(blocks, half)]
  transfers between devices with their start and end apart: 12 -> 9, of which waited for: 7 -> 6; matrix products, arithmetic and copies ran while one was open for 13% -> 7% of each run, Pallas kernels for 0% -> 0%
where the time goes in v2:
time: 56.4 us; the launch traced here: 56 us
  waiting for transfers between devices  13.6 us (24%)
  starting transfers between devices  12.5 us (22%)
  Pallas kernels  10.7 us (19%)
  blocking collectives  10.6 us (19%)
  other arithmetic  4.27 us (8%)
  local copies, waits for them, and re-layouts  3.51 us (6%)
  between operations  0.8 us (1%)
    ppermute x7, starting transfers between devices, spread(): blocks.append(lax.ppermute(x, axis, pairs))  12.4 us
    ppermute x7, waiting for transfers between devices, spread(): blocks.append(lax.ppermute(x, axis, pairs))  11.7 us
    all_to_all x1, blocking collectives, local(): stats = lax.all_to_all(stats, ALL, 0, 0)  10.6 us
    pallas_call x1, Pallas kernels, local(): pl.pallas_call(lambda *refs: head_kernel((rows, half, sections, dps, ys,...  8.79 us
    ppermute x1, waiting for transfers between devices, local(): lax.ppermute(first, 'tensor', pairs)  1.9 us
    pallas_call x1, Pallas kernels, local(): pl.pallas_call(lambda *refs: loss_kernel(own, *refs), out_shape=[jax.Shap...  1.89 us
    unnamed x18, local copies, waits for them, and re-layouts  1.64 us
  transfers between devices with their start and end apart: 9, of which 6 were waited for; matrix products, arithmetic and copies ran while one was open for 7% of the time, Pallas kernels for 0%

profile of v2, /device:TPU:0, one launch (start us, length us, event | category | flops | bytes accessed | tf_op | source)
XLA Modules:
  0.0 56.0 jit_solution(16598194833255815140)
XLA Ops:
  0.6 0.0 copy-start.8
  0.6 0.0 copy-start.4
  0.7 0.0 copy-start.7
  0.7 0.0 copy-start.6
  0.7 0.0 copy-start.5
  0.7 0.7 %select_convert_fusion = bf16[8,128]{1,0:T(8,128)(2,1)S(1)} fusion(s32[128]{0:T(128)S(1)} %maximum_multiply_fusion, s32[8]{0:T(128)} %param.13, pred[128]{0:T(512)(128)(4,1)S(1)} %iota_compare_fusion.1), kind=kLoop, calls=%fused_computation.7 | loop fusion | flops 4096 | bytes 2720 | tf_op jit(solution)/shard_map/convert_element_type | solution.py:201
  1.5 0.8 %pad_maximum_fusion.6 = bf16[8,4224]{1,0:T(8,128)(2,1)S(1)} fusion(bf16[8,128]{1,0:T(8,128)(2,1)S(1)} %select_convert_fusion, bf16[8,4096]{1,0:T(8,128)(2,1)} %param.10), kind=kLoop, calls=%fused_computation.6 | loop fusion | flops 135168 | bytes 135168 | tf_op jit(solution)/shard_map/concatenate | solution.py:203
  2.3 5.1 %collective-permute-start.2 = (bf16[8,4224]{1,0:T(8,128)(2,1)S(1)}, bf16[8,4224]{1,0:T(8,128)(2,1)S(1)}, u32[]{:S(2)}, u32[]{:S(2)}) collective-permute-start(bf16[8,4224]{1,0:T(8,128)(2,1)S(1)} %pad_maximum_fusion.6), channel_id=1, source_target_pairs={{0,24},{8,0},{16,8},{24,16},{1,25},{9,1},{17,9},{25,17},{2,26},{10... | collective-permute-start | bytes 202760 | tf_op jit(solution)/shard_map/ppermute | solution.py:43
  7.4 0.0 collective-permute-start.1
  7.4 1.0 %collective-permute-start = (bf16[8,4224]{1,0:T(8,128)(2,1)S(1)}, bf16[8,4224]{1,0:T(8,128)(2,1)S(1)}, u32[]{:S(2)}, u32[]{:S(2)}) collective-permute-start(bf16[8,4224]{1,0:T(8,128)(2,1)S(1)} %pad_maximum_fusion.6), channel_id=1, source_target_pairs={{0,8},{8,16},{16,24},{24,0},{1,9},{9,17},{17,25},{25,1},{2,10},{10... | collective-permute-start | bytes 202760 | tf_op jit(solution)/shard_map/ppermute | solution.py:43
  8.4 0.9 %select_reduce_fusion = (s32[2]{0:T(128)S(1)}, s32[2]{0:T(128)S(1)}) fusion(s32[2]{0:T(128)} %bitcast.12, s32[2]{0:T(128)S(1)} %and_select_fusion, s32[2]{0:T(128)} %bitcast.13), kind=kLoop, calls=%fused_computation.13 | loop fusion | flops 16 | bytes 40 | tf_op jit(solution)/shard_map/reduce_sum | solution.py:187
  9.3 0.6 %collective-permute-done.2 = bf16[8,4224]{1,0:T(8,128)(2,1)S(1)} collective-permute-done((bf16[8,4224]{1,0:T(8,128)(2,1)S(1)}, bf16[8,4224]{1,0:T(8,128)(2,1)S(1)}, u32[]{:S(2)}, u32[]{:S(2)}) %collective-permute-start.2) | collective-permute-done | bytes 67616 | tf_op jit(solution)/shard_map/ppermute | solution.py:43
  9.9 4.1 %collective-permute-done.1 = bf16[8,4224]{1,0:T(8,128)(2,1)S(1)} collective-permute-done((bf16[8,4224]{1,0:T(8,128)(2,1)S(1)}, bf16[8,4224]{1,0:T(8,128)(2,1)S(1)}, u32[]{:S(2)}, u32[]{:S(2)}) %collective-permute-start.1) | collective-permute-done | bytes 67616 | tf_op jit(solution)/shard_map/ppermute | solution.py:43
  14.0 0.0 collective-permute-done
  14.0 0.9 %pad_maximum_fusion.3 = bf16[32,4224]{1,0:T(8,128)(2,1)S(1)} fusion(bf16[8,4224]{1,0:T(8,128)(2,1)S(1)} %collective-permute-done.2, bf16[8,4224]{1,0:T(8,128)(2,1)S(1)} %collective-permute-done.1, bf16[8,4224]{1,0:T(8,128)(2,1)S(1)} %collective-permute-done, bf16[8,128]{1,0:T(8,128)(2,1)S(1)} %select_convert_fusion, bf16[8,4096]{1,0:T(8,128)(2,1)} %param.10), kind=kLoop, calls=%fused_computation.3 | loop fusion | flops 1351680 | bytes 540672 | tf_op jit(solution)/shard_map/concatenate | solution.py:44
  14.9 1.6 %collective-permute-start.3 = (bf16[32,2176]{1,0:T(8,128)(2,1)S(1)}, bf16[32,2176]{1,0:T(8,128)(2,1)S(1)}, u32[]{:S(2)}, u32[]{:S(2)}) collective-permute-start(bf16[32,2176]{1,0:T(8,128)(2,1)S(1)} %slice.8), channel_id=1, source_target_pairs={{0,2},{1,3},{2,0},{3,1},{4,6},{5,7},{6,4},{7,5},{8,10},{9,11},{10,... | collective-permute-start | bytes 417800 | tf_op jit(solution)/shard_map/ppermute | solution.py:43
  16.5 0.8 %pad_maximum_fusion.5 = bf16[32,2048]{1,0:T(8,128)(2,1)S(1)} fusion(bf16[8,4224]{1,0:T(8,128)(2,1)S(1)} %collective-permute-done.2, bf16[8,4224]{1,0:T(8,128)(2,1)S(1)} %collective-permute-done.1, bf16[8,4224]{1,0:T(8,128)(2,1)S(1)} %collective-permute-done, bf16[8,128]{1,0:T(8,128)(2,1)S(1)} %select_convert_fusion, bf16[8,4096]{1,0:T(8,128)(2,1)} %param.10), kind=kLoop, calls=%fused_computation.5 | loop fusion | flops 655360 | bytes 401408 | tf_op jit(solution)/shard_map/slice | solution.py:204
  17.3 1.6 %collective-permute-start.5 = (bf16[32,2048]{1,0:T(8,128)(2,1)S(1)}, bf16[32,2048]{1,0:T(8,128)(2,1)S(1)}, u32[]{:S(2)}, u32[]{:S(2)}) collective-permute-start(bf16[32,2048]{1,0:T(8,128)(2,1)S(1)} %pad_maximum_fusion.5), channel_id=1, source_target_pairs={{0,4},{4,0},{1,5},{5,1},{2,6},{6,2},{3,7},{7,3},{8,12},{12,8},{9,1... | collective-permute-start | bytes 393224 | tf_op jit(solution)/shard_map/ppermute | solution.py:43
  18.8 1.6 %collective-permute-done.3 = bf16[32,2176]{1,0:T(8,128)(2,1)S(1)} collective-permute-done((bf16[32,2176]{1,0:T(8,128)(2,1)S(1)}, bf16[32,2176]{1,0:T(8,128)(2,1)S(1)}, u32[]{:S(2)}, u32[]{:S(2)}) %collective-permute-start.3) | collective-permute-done | bytes 139296 | tf_op jit(solution)/shard_map/ppermute | solution.py:43
  20.5 1.6 %collective-permute-start.4 = (bf16[64,2176]{1,0:T(8,128)(2,1)S(1)}, bf16[64,2176]{1,0:T(8,128)(2,1)S(1)}, u32[]{:S(2)}, u32[]{:S(2)}) collective-permute-start(bf16[64,2176]{1,0:T(8,128)(2,1)S(1)} %pad_maximum_fusion.2), channel_id=1, source_target_pairs={{0,4},{4,0},{1,5},{5,1},{2,6},{6,2},{3,7},{7,3},{8,12},{12,8},{9,1... | collective-permute-start | bytes 835592 | tf_op jit(solution)/shard_map/ppermute | solution.py:43
  22.1 0.0 copy-done.8
  22.1 0.0 copy-done.4
  22.1 0.6 %reshape.43.refs_5_ = f32[8,2048]{1,0:T(8,128)} reshape(f32[16384]{0:T(1024)S(1)} %copy-done.4) | data formatting | bytes 131072 | tf_op jit(solution)/shard_map/reshape | solution.py:219
  22.7 0.6 %stack.23.refs_0_ = s32[5]{0:T(128)} concatenate(s32[1]{0:T(128)} %bitcast.3, s32[1]{0:T(128)} %bitcast.4, s32[1]{0:T(128)} %bitcast.5, s32[1]{0:T(128)} %bitcast.6, s32[1]{0:T(128)} %bitcast.7), dimensions={0} | concatenate | bytes 40 | tf_op jit(solution)/shard_map/stack | solution.py:209
  23.3 0.0 copy-done.7
  23.3 0.0 copy-done.6
  23.3 0.0 copy-done.5
  23.3 0.6 %concatenate.27 = f32[128]{0:T(128)} concatenate(f32[2]{0:T(128)S(1)} %copy-done.5, f32[2]{0:T(128)S(1)} %copy-done.6, f32[2]{0:T(128)S(1)} %copy-done.7, f32[2]{0:T(128)S(1)} %convert_select_fusion, f32[2]{0:T(128)S(1)} %get-tuple-element.19, f32[2]{0:T(128)S(1)} %convert_element_type.15, f32[116]{0:T(128)S(1)} %broadcast_in_dim.63), dimensions={0} | concatenate | bytes 1024 | tf_op jit(solution)/shard_map/concatenate | solution.py:192
  23.9 0.0 collective-permute-done.5
  24.0 1.6 %collective-permute-start.6 = (bf16[64,2048]{1,0:T(8,128)(2,1)S(1)}, bf16[64,2048]{1,0:T(8,128)(2,1)S(1)}, u32[]{:S(2)}, u32[]{:S(2)}) collective-permute-start(bf16[64,2048]{1,0:T(8,128)(2,1)S(1)} %pad_maximum_fusion.4), channel_id=1, source_target_pairs={{0,2},{1,3},{2,0},{3,1},{4,6},{5,7},{6,4},{7,5},{8,10},{9,11},{10,... | collective-permute-start | bytes 786440 | tf_op jit(solution)/shard_map/ppermute | solution.py:43
  25.6 2.8 %collective-permute-done.4 = bf16[64,2176]{1,0:T(8,128)(2,1)S(1)} collective-permute-done((bf16[64,2176]{1,0:T(8,128)(2,1)S(1)}, bf16[64,2176]{1,0:T(8,128)(2,1)S(1)}, u32[]{:S(2)}, u32[]{:S(2)}) %collective-permute-start.4) | collective-permute-done | bytes 278560 | tf_op jit(solution)/shard_map/ppermute | solution.py:43
  28.4 0.0 copy-start
  28.4 0.1 collective-permute-start.8
  28.5 2.6 %collective-permute-done.6 = bf16[64,2048]{1,0:T(8,128)(2,1)S(1)} collective-permute-done((bf16[64,2048]{1,0:T(8,128)(2,1)S(1)}, bf16[64,2048]{1,0:T(8,128)(2,1)S(1)}, u32[]{:S(2)}, u32[]{:S(2)}) %collective-permute-start.6) | collective-permute-done | bytes 262176 | tf_op jit(solution)/shard_map/ppermute | solution.py:43
  31.1 0.0 copy-start.1
  31.1 0.1 collective-permute-start.7
  31.2 1.9 %collective-permute-done.7.refs_3_ = bf16[128,2048]{1,0:T(8,128)(2,1)S(1)} collective-permute-done((bf16[128,2048]{1,0:T(8,128)(2,1)S(1)}, bf16[128,2048]{1,0:T(8,128)(2,1)S(1)}, u32[]{:S(2)}, u32[]{:S(2)}) %collective-permute-start.7) | collective-permute-done | bytes 524320 | tf_op jit(solution)/shard_map/ppermute | solution.py:224
  33.1 0.0 copy-start.3
  33.1 0.0 collective-permute-done.8.refs_4_
  33.1 0.0 copy-done
  33.1 0.0 copy-done.1
  33.1 0.8 %copy-done.3 = bf16[128,2048]{1,0:T(8,128)(2,1)} copy-done((bf16[128,2048]{1,0:T(8,128)(2,1)}, bf16[128,2048]{1,0:T(8,128)(2,1)S(1)}, u32[]{:S(2)}) %copy-start.3) | copy-done | bytes 524312
  33.9 0.0 copy-start.2
  33.9 0.8 %copy-done.2 = bf16[128,2176]{1,0:T(8,128)(2,1)} copy-done((bf16[128,2176]{1,0:T(8,128)(2,1)}, bf16[128,2176]{1,0:T(8,128)(2,1)S(1)}, u32[]{:S(2)}) %copy-start.2) | copy-done | bytes 557080
  34.7 8.8 %shard_map.121 = f32[32,1,320]{2,1,0:T(1,128)} custom-call(s32[5]{0:T(128)} %stack.23.refs_0_, bf16[128,2048]{1,0:T(8,128)(2,1)} %copy-done.1, bf16[128,2176]{1,0:T(8,128)(2,1)} %copy-done, bf16[128,2048]{1,0:T(8,128)(2,1)} %copy-done.3, bf16[128,2176]{1,0:T(8,128)(2,1)} %copy-done.2, f32[8,2048]{1,0:T(8,128)} %reshape.43.refs_5_, f32[1,128]{1,0:T(1,128)} %bitcast.11, ...), custom_call_target="tpu_custom_call" | custom-call | tf_op jit(solution)/shard_map/pallas_call | solution.py:230
  43.5 10.6 %all_to_all.5.refs_1_ = f32[32,1,320]{2,1,0:T(1,128)} all-to-all(f32[32,1,320]{2,1,0:T(1,128)} %shard_map.121), channel_id=1, replica_groups=mesh['section'=4,'dp'=2,'tensor'=4] {'section','dp','tensor'}, dimensions={0} | all-to-all | bytes 81920 | tf_op jit(solution)/shard_map/all_to_all | solution.py:241
  54.1 1.9 %shard_map.122 = (f32[1,2]{1,0:T(1,128)}, f32[1,8]{1,0:T(1,128)}, f32[1,8]{1,0:T(1,128)}) custom-call(s32[5]{0:T(128)} %stack.23.refs_0_, f32[32,1,320]{2,1,0:T(1,128)} %all_to_all.5.refs_1_), custom_call_target="tpu_custom_call" | custom-call | tf_op jit(solution)/shard_map/pallas_call | solution.py:242
  (12 shorter events, 0.2 us)
Async XLA Ops:
  0.6 21.4 %copy-start.8 = (s32[2]{0:T(128)S(1)}, s32[2]{0:T(128)}, u32[]{:S(2)}) copy-start(s32[2]{0:T(128)} %param.16) | copy-start | bytes 28
  0.6 21.4 %copy-start.4 = (f32[16384]{0:T(1024)S(1)}, f32[16384]{0:T(1024)}, u32[]{:S(2)}) copy-start(f32[16384]{0:T(1024)} %param.11) | copy-start | bytes 196612
  0.7 22.7 %copy-start.7 = (f32[2]{0:T(128)S(1)}, f32[2]{0:T(128)}, u32[]{:S(2)}) copy-start(f32[2]{0:T(128)} %param.19) | copy-start | bytes 28
  0.7 22.7 %copy-start.6 = (f32[2]{0:T(128)S(1)}, f32[2]{0:T(128)}, u32[]{:S(2)}) copy-start(f32[2]{0:T(128)} %param.18) | copy-start | bytes 28
  0.7 22.7 %copy-start.5 = (f32[2]{0:T(128)S(1)}, f32[2]{0:T(128)}, u32[]{:S(2)}) copy-start(f32[2]{0:T(128)} %param.17) | copy-start | bytes 28
  2.3 7.6 %collective-permute-start.2 = (bf16[8,4224]{1,0:T(8,128)(2,1)S(1)}, bf16[8,4224]{1,0:T(8,128)(2,1)S(1)}, u32[]{:S(2)}, u32[]{:S(2)}) collective-permute-start(bf16[8,4224]{1,0:T(8,128)(2,1)S(1)} %pad_maximum_fusion.6), channel_id=1, source_target_pairs={{0,24},{8,0},{16,8},{24,16},{1,25},{9,1},{17,9},{25,17},{2,26},{10... | collective-permute-start | bytes 202760 | tf_op jit(solution)/shard_map/ppermute | solution.py:43
  7.4 6.6 %collective-permute-start.1 = (bf16[8,4224]{1,0:T(8,128)(2,1)S(1)}, bf16[8,4224]{1,0:T(8,128)(2,1)S(1)}, u32[]{:S(2)}, u32[]{:S(2)}) collective-permute-start(bf16[8,4224]{1,0:T(8,128)(2,1)S(1)} %pad_maximum_fusion.6), channel_id=1, source_target_pairs={{0,16},{8,24},{16,0},{24,8},{1,17},{9,25},{17,1},{25,9},{2,18},{10... | collective-permute-start | bytes 202760 | tf_op jit(solution)/shard_map/ppermute | solution.py:43
  7.4 6.6 %collective-permute-start = (bf16[8,4224]{1,0:T(8,128)(2,1)S(1)}, bf16[8,4224]{1,0:T(8,128)(2,1)S(1)}, u32[]{:S(2)}, u32[]{:S(2)}) collective-permute-start(bf16[8,4224]{1,0:T(8,128)(2,1)S(1)} %pad_maximum_fusion.6), channel_id=1, source_target_pairs={{0,8},{8,16},{16,24},{24,0},{1,9},{9,17},{17,25},{25,1},{2,10},{10... | collective-permute-start | bytes 202760 | tf_op jit(solution)/shard_map/ppermute | solution.py:43
  14.9 5.6 %collective-permute-start.3 = (bf16[32,2176]{1,0:T(8,128)(2,1)S(1)}, bf16[32,2176]{1,0:T(8,128)(2,1)S(1)}, u32[]{:S(2)}, u32[]{:S(2)}) collective-permute-start(bf16[32,2176]{1,0:T(8,128)(2,1)S(1)} %slice.8), channel_id=1, source_target_pairs={{0,2},{1,3},{2,0},{3,1},{4,6},{5,7},{6,4},{7,5},{8,10},{9,11},{10,... | collective-permute-start | bytes 417800 | tf_op jit(solution)/shard_map/ppermute | solution.py:43
  17.3 6.7 %collective-permute-start.5 = (bf16[32,2048]{1,0:T(8,128)(2,1)S(1)}, bf16[32,2048]{1,0:T(8,128)(2,1)S(1)}, u32[]{:S(2)}, u32[]{:S(2)}) collective-permute-start(bf16[32,2048]{1,0:T(8,128)(2,1)S(1)} %pad_maximum_fusion.5), channel_id=1, source_target_pairs={{0,4},{4,0},{1,5},{5,1},{2,6},{6,2},{3,7},{7,3},{8,12},{12,8},{9,1... | collective-permute-start | bytes 393224 | tf_op jit(solution)/shard_map/ppermute | solution.py:43
  20.5 7.8 %collective-permute-start.4 = (bf16[64,2176]{1,0:T(8,128)(2,1)S(1)}, bf16[64,2176]{1,0:T(8,128)(2,1)S(1)}, u32[]{:S(2)}, u32[]{:S(2)}) collective-permute-start(bf16[64,2176]{1,0:T(8,128)(2,1)S(1)} %pad_maximum_fusion.2), channel_id=1, source_target_pairs={{0,4},{4,0},{1,5},{5,1},{2,6},{6,2},{3,7},{7,3},{8,12},{12,8},{9,1... | collective-permute-start | bytes 835592 | tf_op jit(solution)/shard_map/ppermute | solution.py:43
  24.0 7.1 %collective-permute-start.6 = (bf16[64,2048]{1,0:T(8,128)(2,1)S(1)}, bf16[64,2048]{1,0:T(8,128)(2,1)S(1)}, u32[]{:S(2)}, u32[]{:S(2)}) collective-permute-start(bf16[64,2048]{1,0:T(8,128)(2,1)S(1)} %pad_maximum_fusion.4), channel_id=1, source_target_pairs={{0,2},{1,3},{2,0},{3,1},{4,6},{5,7},{6,4},{7,5},{8,10},{9,11},{10,... | collective-permute-start | bytes 786440 | tf_op jit(solution)/shard_map/ppermute | solution.py:43
  28.4 4.7 %copy-start = (bf16[128,2176]{1,0:T(8,128)(2,1)}, bf16[128,2176]{1,0:T(8,128)(2,1)S(1)}, u32[]{:S(2)}) copy-start(bf16[128,2176]{1,0:T(8,128)(2,1)S(1)} %pad_maximum_fusion.refs_2_) | copy-start | bytes 1671172
  28.4 4.7 %collective-permute-start.8 = (bf16[128,2176]{1,0:T(8,128)(2,1)S(1)}, bf16[128,2176]{1,0:T(8,128)(2,1)S(1)}, u32[]{:S(2)}, u32[]{:S(2)}) collective-permute-start(bf16[128,2176]{1,0:T(8,128)(2,1)S(1)} %pad_maximum_fusion.refs_2_), channel_id=1, source_target_pairs={{0,1},{1,0},{2,3},{3,2},{4,5},{5,4},{6,7},{7,6},{8,9},{9,8},{10,11... | collective-permute-start | bytes 1671176 | tf_op jit(solution)/shard_map/ppermute | solution.py:224
  31.1 2.0 %copy-start.1 = (bf16[128,2048]{1,0:T(8,128)(2,1)}, bf16[128,2048]{1,0:T(8,128)(2,1)S(1)}, u32[]{:S(2)}) copy-start(bf16[128,2048]{1,0:T(8,128)(2,1)S(1)} %pad_maximum_fusion.1.refs_1_) | copy-start | bytes 1572868
  31.1 2.0 %collective-permute-start.7 = (bf16[128,2048]{1,0:T(8,128)(2,1)S(1)}, bf16[128,2048]{1,0:T(8,128)(2,1)S(1)}, u32[]{:S(2)}, u32[]{:S(2)}) collective-permute-start(bf16[128,2048]{1,0:T(8,128)(2,1)S(1)} %pad_maximum_fusion.1.refs_1_), channel_id=1, source_target_pairs={{0,1},{1,0},{2,3},{3,2},{4,5},{5,4},{6,7},{7,6},{8,9},{9,8},{10,11... | collective-permute-start | bytes 1572872 | tf_op jit(solution)/shard_map/ppermute | solution.py:224
  33.1 0.8 %copy-start.3 = (bf16[128,2048]{1,0:T(8,128)(2,1)}, bf16[128,2048]{1,0:T(8,128)(2,1)S(1)}, u32[]{:S(2)}) copy-start(bf16[128,2048]{1,0:T(8,128)(2,1)S(1)} %collective-permute-done.7.refs_3_) | copy-start | bytes 1572868
  33.9 0.8 %copy-start.2 = (bf16[128,2176]{1,0:T(8,128)(2,1)}, bf16[128,2176]{1,0:T(8,128)(2,1)S(1)}, u32[]{:S(2)}) copy-start(bf16[128,2176]{1,0:T(8,128)(2,1)S(1)} %collective-permute-done.8.refs_4_) | copy-start | bytes 1671172

commit v3 on v2

--- a/solution.py
+++ b/solution.py
@@ -10,6 +10,7 @@
 FIELDS = 6
 DIGITS = 3
 BITS = 8
+VMEM_BYTES = 2**22
 
 epsilon = 1e-05
 clip_range = 0.2
@@ -227,6 +228,8 @@
     vocab = head_weight.shape[0]
     vmem = pl.BlockSpec(memory_space=pltpu.VMEM)
     smem = pl.BlockSpec(memory_space=pltpu.SMEM)
+    if sum(piece.size * piece.dtype.itemsize for piece in pieces) <= VMEM_BYTES:
+        pieces = [pltpu.with_memory_space_constraint(piece, pltpu.VMEM) for piece in pieces]
     stats = pl.pallas_call(
         lambda *refs: head_kernel((rows, half, sections, dps, ys, cores), *refs),
         out_shape=jax.ShapeDtypeStruct((devices, 1, 3 * tok + extra_width), jnp.float32),

time: 56.4 us -> 54.1 us (0.959)
  local copies, waits for them, and re-layouts: 3.51 us -> 1.94 us
  Pallas kernels: 10.7 us -> 9.99 us
    unnamed x18 -> x10, local copies, waits for them, and re-layouts: 1.64 us -> 0.02 us
    pallas_call x1, Pallas kernels: 8.79 us -> 8.1 us  [local(): pl.pallas_call(lambda *refs: head_kernel((rows, half, sections, dps, ys,...]
where the time goes in v3:
time: 54.1 us; the launch traced here: 53.7 us
  waiting for transfers between devices  13.6 us (25%)
  starting transfers between devices  12.5 us (23%)
  blocking collectives  10.6 us (20%)
  Pallas kernels  9.99 us (18%)
  other arithmetic  4.27 us (8%)
  local copies, waits for them, and re-layouts  1.94 us (4%)
  between operations  0.77 us (1%)
    ppermute x7, starting transfers between devices, spread(): blocks.append(lax.ppermute(x, axis, pairs))  12.4 us
    ppermute x7, waiting for transfers between devices, spread(): blocks.append(lax.ppermute(x, axis, pairs))  11.7 us
    all_to_all x1, blocking collectives, local(): stats = lax.all_to_all(stats, ALL, 0, 0)  10.6 us
    pallas_call x1, Pallas kernels, local(): pl.pallas_call(lambda *refs: head_kernel((rows, half, sections, dps, ys,...  8.1 us
    ppermute x1, waiting for transfers between devices, local(): lax.ppermute(first, 'tensor', pairs)  1.9 us
    pallas_call x1, Pallas kernels, local(): pl.pallas_call(lambda *refs: loss_kernel(own, *refs), out_shape=[jax.Shap...  1.89 us
  transfers between devices with their start and end apart: 9, of which 6 were waited for; matrix products, arithmetic and copies ran while one was open for 7% of the time, Pallas kernels for 0%

profile of v3, /device:TPU:0, one launch (start us, length us, event | category | flops | bytes accessed | tf_op | source)
XLA Modules:
  0.0 53.7 jit_solution(13768664407105150080)
XLA Ops:
  0.6 0.0 copy-start.4
  0.6 0.0 copy-start
  0.7 0.0 copy-start.3
  0.7 0.0 copy-start.2
  0.7 0.0 copy-start.1
  0.7 0.7 %select_convert_fusion = bf16[8,128]{1,0:T(8,128)(2,1)S(1)} fusion(s32[128]{0:T(128)S(1)} %maximum_multiply_fusion, s32[8]{0:T(128)} %param.13, pred[128]{0:T(512)(128)(4,1)S(1)} %iota_compare_fusion.1), kind=kLoop, calls=%fused_computation.7 | loop fusion | flops 4096 | bytes 2720 | tf_op jit(solution)/shard_map/convert_element_type | solution.py:202
  1.5 0.8 %pad_maximum_fusion.6 = bf16[8,4224]{1,0:T(8,128)(2,1)S(1)} fusion(bf16[8,128]{1,0:T(8,128)(2,1)S(1)} %select_convert_fusion, bf16[8,4096]{1,0:T(8,128)(2,1)} %param.10), kind=kLoop, calls=%fused_computation.6 | loop fusion | flops 135168 | bytes 135168 | tf_op jit(solution)/shard_map/concatenate | solution.py:204
  2.3 5.1 %collective-permute-start.2 = (bf16[8,4224]{1,0:T(8,128)(2,1)S(1)}, bf16[8,4224]{1,0:T(8,128)(2,1)S(1)}, u32[]{:S(2)}, u32[]{:S(2)}) collective-permute-start(bf16[8,4224]{1,0:T(8,128)(2,1)S(1)} %pad_maximum_fusion.6), channel_id=1, source_target_pairs={{0,24},{8,0},{16,8},{24,16},{1,25},{9,1},{17,9},{25,17},{2,26},{10... | collective-permute-start | bytes 202760 | tf_op jit(solution)/shard_map/ppermute | solution.py:44
  7.4 0.0 collective-permute-start.1
  7.4 1.0 %collective-permute-start = (bf16[8,4224]{1,0:T(8,128)(2,1)S(1)}, bf16[8,4224]{1,0:T(8,128)(2,1)S(1)}, u32[]{:S(2)}, u32[]{:S(2)}) collective-permute-start(bf16[8,4224]{1,0:T(8,128)(2,1)S(1)} %pad_maximum_fusion.6), channel_id=1, source_target_pairs={{0,8},{8,16},{16,24},{24,0},{1,9},{9,17},{17,25},{25,1},{2,10},{10... | collective-permute-start | bytes 202760 | tf_op jit(solution)/shard_map/ppermute | solution.py:44
  8.4 0.9 %select_reduce_fusion = (s32[2]{0:T(128)S(1)}, s32[2]{0:T(128)S(1)}) fusion(s32[2]{0:T(128)} %bitcast.12, s32[2]{0:T(128)S(1)} %and_select_fusion, s32[2]{0:T(128)} %bitcast.13), kind=kLoop, calls=%fused_computation.13 | loop fusion | flops 16 | bytes 40 | tf_op jit(solution)/shard_map/reduce_sum | solution.py:188
  9.3 0.6 %collective-permute-done.2 = bf16[8,4224]{1,0:T(8,128)(2,1)S(1)} collective-permute-done((bf16[8,4224]{1,0:T(8,128)(2,1)S(1)}, bf16[8,4224]{1,0:T(8,128)(2,1)S(1)}, u32[]{:S(2)}, u32[]{:S(2)}) %collective-permute-start.2) | collective-permute-done | bytes 67616 | tf_op jit(solution)/shard_map/ppermute | solution.py:44
  9.9 4.1 %collective-permute-done.1 = bf16[8,4224]{1,0:T(8,128)(2,1)S(1)} collective-permute-done((bf16[8,4224]{1,0:T(8,128)(2,1)S(1)}, bf16[8,4224]{1,0:T(8,128)(2,1)S(1)}, u32[]{:S(2)}, u32[]{:S(2)}) %collective-permute-start.1) | collective-permute-done | bytes 67616 | tf_op jit(solution)/shard_map/ppermute | solution.py:44
  14.0 0.0 collective-permute-done
  14.0 0.9 %pad_maximum_fusion.3 = bf16[32,4224]{1,0:T(8,128)(2,1)S(1)} fusion(bf16[8,4224]{1,0:T(8,128)(2,1)S(1)} %collective-permute-done.2, bf16[8,4224]{1,0:T(8,128)(2,1)S(1)} %collective-permute-done.1, bf16[8,4224]{1,0:T(8,128)(2,1)S(1)} %collective-permute-done, bf16[8,128]{1,0:T(8,128)(2,1)S(1)} %select_convert_fusion, bf16[8,4096]{1,0:T(8,128)(2,1)} %param.10), kind=kLoop, calls=%fused_computation.3 | loop fusion | flops 1351680 | bytes 540672 | tf_op jit(solution)/shard_map/concatenate | solution.py:45
  14.9 1.6 %collective-permute-start.3 = (bf16[32,2176]{1,0:T(8,128)(2,1)S(1)}, bf16[32,2176]{1,0:T(8,128)(2,1)S(1)}, u32[]{:S(2)}, u32[]{:S(2)}) collective-permute-start(bf16[32,2176]{1,0:T(8,128)(2,1)S(1)} %slice.8), channel_id=1, source_target_pairs={{0,2},{1,3},{2,0},{3,1},{4,6},{5,7},{6,4},{7,5},{8,10},{9,11},{10,... | collective-permute-start | bytes 417800 | tf_op jit(solution)/shard_map/ppermute | solution.py:44
  16.5 0.8 %pad_maximum_fusion.5 = bf16[32,2048]{1,0:T(8,128)(2,1)S(1)} fusion(bf16[8,4224]{1,0:T(8,128)(2,1)S(1)} %collective-permute-done.2, bf16[8,4224]{1,0:T(8,128)(2,1)S(1)} %collective-permute-done.1, bf16[8,4224]{1,0:T(8,128)(2,1)S(1)} %collective-permute-done, bf16[8,128]{1,0:T(8,128)(2,1)S(1)} %select_convert_fusion, bf16[8,4096]{1,0:T(8,128)(2,1)} %param.10), kind=kLoop, calls=%fused_computation.5 | loop fusion | flops 655360 | bytes 401408 | tf_op jit(solution)/shard_map/slice | solution.py:205
  17.3 1.6 %collective-permute-start.5 = (bf16[32,2048]{1,0:T(8,128)(2,1)S(1)}, bf16[32,2048]{1,0:T(8,128)(2,1)S(1)}, u32[]{:S(2)}, u32[]{:S(2)}) collective-permute-start(bf16[32,2048]{1,0:T(8,128)(2,1)S(1)} %pad_maximum_fusion.5), channel_id=1, source_target_pairs={{0,4},{4,0},{1,5},{5,1},{2,6},{6,2},{3,7},{7,3},{8,12},{12,8},{9,1... | collective-permute-start | bytes 393224 | tf_op jit(solution)/shard_map/ppermute | solution.py:44
  18.8 1.6 %collective-permute-done.3 = bf16[32,2176]{1,0:T(8,128)(2,1)S(1)} collective-permute-done((bf16[32,2176]{1,0:T(8,128)(2,1)S(1)}, bf16[32,2176]{1,0:T(8,128)(2,1)S(1)}, u32[]{:S(2)}, u32[]{:S(2)}) %collective-permute-start.3) | collective-permute-done | bytes 139296 | tf_op jit(solution)/shard_map/ppermute | solution.py:44
  20.5 1.6 %collective-permute-start.4 = (bf16[64,2176]{1,0:T(8,128)(2,1)S(1)}, bf16[64,2176]{1,0:T(8,128)(2,1)S(1)}, u32[]{:S(2)}, u32[]{:S(2)}) collective-permute-start(bf16[64,2176]{1,0:T(8,128)(2,1)S(1)} %pad_maximum_fusion.2), channel_id=1, source_target_pairs={{0,4},{4,0},{1,5},{5,1},{2,6},{6,2},{3,7},{7,3},{8,12},{12,8},{9,1... | collective-permute-start | bytes 835592 | tf_op jit(solution)/shard_map/ppermute | solution.py:44
  22.1 0.0 copy-done.4
  22.1 0.0 copy-done
  22.1 0.6 %reshape.43.refs_5_ = f32[8,2048]{1,0:T(8,128)} reshape(f32[16384]{0:T(1024)S(1)} %copy-done) | data formatting | bytes 131072 | tf_op jit(solution)/shard_map/reshape | solution.py:220
  22.7 0.7 %stack.23.refs_0_ = s32[5]{0:T(128)} concatenate(s32[1]{0:T(128)} %bitcast.3, s32[1]{0:T(128)} %bitcast.4, s32[1]{0:T(128)} %bitcast.5, s32[1]{0:T(128)} %bitcast.6, s32[1]{0:T(128)} %bitcast.7), dimensions={0} | concatenate | bytes 40 | tf_op jit(solution)/shard_map/stack | solution.py:210
  23.4 0.0 copy-done.3
  23.4 0.0 copy-done.2
  23.4 0.0 copy-done.1
  23.4 0.6 %concatenate.27 = f32[128]{0:T(128)} concatenate(f32[2]{0:T(128)S(1)} %copy-done.1, f32[2]{0:T(128)S(1)} %copy-done.2, f32[2]{0:T(128)S(1)} %copy-done.3, f32[2]{0:T(128)S(1)} %convert_select_fusion, f32[2]{0:T(128)S(1)} %get-tuple-element.19, f32[2]{0:T(128)S(1)} %convert_element_type.15, f32[116]{0:T(128)S(1)} %broadcast_in_dim.63), dimensions={0} | concatenate | bytes 1024 | tf_op jit(solution)/shard_map/concatenate | solution.py:193
  24.0 0.0 collective-permute-done.5
  24.0 1.6 %collective-permute-start.6 = (bf16[64,2048]{1,0:T(8,128)(2,1)S(1)}, bf16[64,2048]{1,0:T(8,128)(2,1)S(1)}, u32[]{:S(2)}, u32[]{:S(2)}) collective-permute-start(bf16[64,2048]{1,0:T(8,128)(2,1)S(1)} %pad_maximum_fusion.4), channel_id=1, source_target_pairs={{0,2},{1,3},{2,0},{3,1},{4,6},{5,7},{6,4},{7,5},{8,10},{9,11},{10,... | collective-permute-start | bytes 786440 | tf_op jit(solution)/shard_map/ppermute | solution.py:44
  25.6 2.7 %collective-permute-done.4 = bf16[64,2176]{1,0:T(8,128)(2,1)S(1)} collective-permute-done((bf16[64,2176]{1,0:T(8,128)(2,1)S(1)}, bf16[64,2176]{1,0:T(8,128)(2,1)S(1)}, u32[]{:S(2)}, u32[]{:S(2)}) %collective-permute-start.4) | collective-permute-done | bytes 278560 | tf_op jit(solution)/shard_map/ppermute | solution.py:44
  28.4 0.1 collective-permute-start.8
  28.5 2.6 %collective-permute-done.6 = bf16[64,2048]{1,0:T(8,128)(2,1)S(1)} collective-permute-done((bf16[64,2048]{1,0:T(8,128)(2,1)S(1)}, bf16[64,2048]{1,0:T(8,128)(2,1)S(1)}, u32[]{:S(2)}, u32[]{:S(2)}) %collective-permute-start.6) | collective-permute-done | bytes 262176 | tf_op jit(solution)/shard_map/ppermute | solution.py:44
  31.1 0.1 collective-permute-start.7
  31.2 1.9 %collective-permute-done.7.refs_3_ = bf16[128,2048]{1,0:T(8,128)(2,1)S(1)} collective-permute-done((bf16[128,2048]{1,0:T(8,128)(2,1)S(1)}, bf16[128,2048]{1,0:T(8,128)(2,1)S(1)}, u32[]{:S(2)}, u32[]{:S(2)}) %collective-permute-start.7) | collective-permute-done | bytes 524320 | tf_op jit(solution)/shard_map/ppermute | solution.py:225
  33.1 0.0 collective-permute-done.8.refs_4_
  33.1 8.1 %shard_map.121 = f32[32,1,320]{2,1,0:T(1,128)} custom-call(s32[5]{0:T(128)} %stack.23.refs_0_, bf16[128,2048]{1,0:T(8,128)(2,1)S(1)} %pad_maximum_fusion.1.refs_1_, bf16[128,2176]{1,0:T(8,128)(2,1)S(1)} %pad_maximum_fusion.refs_2_, bf16[128,2048]{1,0:T(8,128)(2,1)S(1)} %collective-permute-done.7.refs_3_, ...), custom_call_target="tpu_custom_call" | custom-call | tf_op jit(solution)/shard_map/pallas_call | solution.py:233
  41.2 10.6 %all_to_all.5.refs_1_ = f32[32,1,320]{2,1,0:T(1,128)} all-to-all(f32[32,1,320]{2,1,0:T(1,128)} %shard_map.121), channel_id=1, replica_groups=mesh['section'=4,'dp'=2,'tensor'=4] {'section','dp','tensor'}, dimensions={0} | all-to-all | bytes 81920 | tf_op jit(solution)/shard_map/all_to_all | solution.py:244
  51.8 1.9 %shard_map.122 = (f32[1,2]{1,0:T(1,128)}, f32[1,8]{1,0:T(1,128)}, f32[1,8]{1,0:T(1,128)}) custom-call(s32[5]{0:T(128)} %stack.23.refs_0_, f32[32,1,320]{2,1,0:T(1,128)} %all_to_all.5.refs_1_), custom_call_target="tpu_custom_call" | custom-call | tf_op jit(solution)/shard_map/pallas_call | solution.py:245
  (12 shorter events, 0.2 us)
Async XLA Ops:
  0.6 21.4 %copy-start.4 = (s32[2]{0:T(128)S(1)}, s32[2]{0:T(128)}, u32[]{:S(2)}) copy-start(s32[2]{0:T(128)} %param.16) | copy-start | bytes 28
  0.6 21.4 %copy-start = (f32[16384]{0:T(1024)S(1)}, f32[16384]{0:T(1024)}, u32[]{:S(2)}) copy-start(f32[16384]{0:T(1024)} %param.11) | copy-start | bytes 196612
  0.7 22.7 %copy-start.3 = (f32[2]{0:T(128)S(1)}, f32[2]{0:T(128)}, u32[]{:S(2)}) copy-start(f32[2]{0:T(128)} %param.19) | copy-start | bytes 28
  0.7 22.7 %copy-start.2 = (f32[2]{0:T(128)S(1)}, f32[2]{0:T(128)}, u32[]{:S(2)}) copy-start(f32[2]{0:T(128)} %param.18) | copy-start | bytes 28
  0.7 22.7 %copy-start.1 = (f32[2]{0:T(128)S(1)}, f32[2]{0:T(128)}, u32[]{:S(2)}) copy-start(f32[2]{0:T(128)} %param.17) | copy-start | bytes 28
  2.3 7.6 %collective-permute-start.2 = (bf16[8,4224]{1,0:T(8,128)(2,1)S(1)}, bf16[8,4224]{1,0:T(8,128)(2,1)S(1)}, u32[]{:S(2)}, u32[]{:S(2)}) collective-permute-start(bf16[8,4224]{1,0:T(8,128)(2,1)S(1)} %pad_maximum_fusion.6), channel_id=1, source_target_pairs={{0,24},{8,0},{16,8},{24,16},{1,25},{9,1},{17,9},{25,17},{2,26},{10... | collective-permute-start | bytes 202760 | tf_op jit(solution)/shard_map/ppermute | solution.py:44
  7.4 6.6 %collective-permute-start.1 = (bf16[8,4224]{1,0:T(8,128)(2,1)S(1)}, bf16[8,4224]{1,0:T(8,128)(2,1)S(1)}, u32[]{:S(2)}, u32[]{:S(2)}) collective-permute-start(bf16[8,4224]{1,0:T(8,128)(2,1)S(1)} %pad_maximum_fusion.6), channel_id=1, source_target_pairs={{0,16},{8,24},{16,0},{24,8},{1,17},{9,25},{17,1},{25,9},{2,18},{10... | collective-permute-start | bytes 202760 | tf_op jit(solution)/shard_map/ppermute | solution.py:44
  7.4 6.6 %collective-permute-start = (bf16[8,4224]{1,0:T(8,128)(2,1)S(1)}, bf16[8,4224]{1,0:T(8,128)(2,1)S(1)}, u32[]{:S(2)}, u32[]{:S(2)}) collective-permute-start(bf16[8,4224]{1,0:T(8,128)(2,1)S(1)} %pad_maximum_fusion.6), channel_id=1, source_target_pairs={{0,8},{8,16},{16,24},{24,0},{1,9},{9,17},{17,25},{25,1},{2,10},{10... | collective-permute-start | bytes 202760 | tf_op jit(solution)/shard_map/ppermute | solution.py:44
  14.9 5.6 %collective-permute-start.3 = (bf16[32,2176]{1,0:T(8,128)(2,1)S(1)}, bf16[32,2176]{1,0:T(8,128)(2,1)S(1)}, u32[]{:S(2)}, u32[]{:S(2)}) collective-permute-start(bf16[32,2176]{1,0:T(8,128)(2,1)S(1)} %slice.8), channel_id=1, source_target_pairs={{0,2},{1,3},{2,0},{3,1},{4,6},{5,7},{6,4},{7,5},{8,10},{9,11},{10,... | collective-permute-start | bytes 417800 | tf_op jit(solution)/shard_map/ppermute | solution.py:44
  17.3 6.7 %collective-permute-start.5 = (bf16[32,2048]{1,0:T(8,128)(2,1)S(1)}, bf16[32,2048]{1,0:T(8,128)(2,1)S(1)}, u32[]{:S(2)}, u32[]{:S(2)}) collective-permute-start(bf16[32,2048]{1,0:T(8,128)(2,1)S(1)} %pad_maximum_fusion.5), channel_id=1, source_target_pairs={{0,4},{4,0},{1,5},{5,1},{2,6},{6,2},{3,7},{7,3},{8,12},{12,8},{9,1... | collective-permute-start | bytes 393224 | tf_op jit(solution)/shard_map/ppermute | solution.py:44
  20.5 7.8 %collective-permute-start.4 = (bf16[64,2176]{1,0:T(8,128)(2,1)S(1)}, bf16[64,2176]{1,0:T(8,128)(2,1)S(1)}, u32[]{:S(2)}, u32[]{:S(2)}) collective-permute-start(bf16[64,2176]{1,0:T(8,128)(2,1)S(1)} %pad_maximum_fusion.2), channel_id=1, source_target_pairs={{0,4},{4,0},{1,5},{5,1},{2,6},{6,2},{3,7},{7,3},{8,12},{12,8},{9,1... | collective-permute-start | bytes 835592 | tf_op jit(solution)/shard_map/ppermute | solution.py:44
  24.0 7.1 %collective-permute-start.6 = (bf16[64,2048]{1,0:T(8,128)(2,1)S(1)}, bf16[64,2048]{1,0:T(8,128)(2,1)S(1)}, u32[]{:S(2)}, u32[]{:S(2)}) collective-permute-start(bf16[64,2048]{1,0:T(8,128)(2,1)S(1)} %pad_maximum_fusion.4), channel_id=1, source_target_pairs={{0,2},{1,3},{2,0},{3,1},{4,6},{5,7},{6,4},{7,5},{8,10},{9,11},{10,... | collective-permute-start | bytes 786440 | tf_op jit(solution)/shard_map/ppermute | solution.py:44
  28.4 4.7 %collective-permute-start.8 = (bf16[128,2176]{1,0:T(8,128)(2,1)S(1)}, bf16[128,2176]{1,0:T(8,128)(2,1)S(1)}, u32[]{:S(2)}, u32[]{:S(2)}) collective-permute-start(bf16[128,2176]{1,0:T(8,128)(2,1)S(1)} %pad_maximum_fusion.refs_2_), channel_id=1, source_target_pairs={{0,1},{1,0},{2,3},{3,2},{4,5},{5,4},{6,7},{7,6},{8,9},{9,8},{10,11... | collective-permute-start | bytes 1671176 | tf_op jit(solution)/shard_map/ppermute | solution.py:225
  31.1 2.0 %collective-permute-start.7 = (bf16[128,2048]{1,0:T(8,128)(2,1)S(1)}, bf16[128,2048]{1,0:T(8,128)(2,1)S(1)}, u32[]{:S(2)}, u32[]{:S(2)}) collective-permute-start(bf16[128,2048]{1,0:T(8,128)(2,1)S(1)} %pad_maximum_fusion.1.refs_1_), channel_id=1, source_target_pairs={{0,1},{1,0},{2,3},{3,2},{4,5},{5,4},{6,7},{7,6},{8,9},{9,8},{10,11... | collective-permute-start | bytes 1572872 | tf_op jit(solution)/shard_map/ppermute | solution.py:225
